TPU v7x, 512 devices: a whole 4x8x8 slice. The times are simulated.
512 devices in a mesh: halo: 8 (over x, core), leaf: 64 (over y, z).
Axes of the slice: x: 4, y: 8, z: 8, core: 2. Of those that a mesh axis runs over, the one named last changes fastest.
Arguments:
- start_modes: bfloat16 [64, 128, 32, 4, 128], P('leaf', None, 'halo'), may hold values from -6 to 6
- density: float32 [64, 32, 4, 128], P('leaf', 'halo'), may hold values from 0.5 to 4
- planes: int32 [64], P('leaf'), may hold values from 1 to 32, 1071 in all
- tree_order: int32 [64], replicated, may hold values from 0 to 63, each once
- iface_index: int32 [64, 2, 128], P('leaf', None, 'halo'), may hold values from 0 to 2047
- iface_stiff: float32 [64, 2, 128], P('leaf', None, 'halo'), may hold values from 0.5 to 2
- reduced_start: float32 [384, 128], replicated, may hold values from -6 to 6
Outputs:
- modes: float32 [64, 128, 32, 4, 128], P('leaf', None, 'halo')
- reduced: float32 [64, 128, 128], P('leaf')
All inputs are finite; a program needn't handle non-finite values. No bound on the sum of `planes` on one device may be relied on, other than what follows from the above.
Results may differ from a plain program's by a relative error of at most 0.0003.
Values sent between devices are 32-bit elements; how exact they have to be, the bound alone decides.
No kernel may reach another device: no remote copies, remote signals or barrier semaphores. Data moves between devices by JAX's collectives and lax.ppermute only.
A program may use at most 64 MiB of HBM per device.

v0:
```python
import math

import jax
import jax.numpy as jnp
from jax import lax
from jax.sharding import PartitionSpec as P

RITERS = 2
LEVELS = 2


EXACT = lax.Precision.HIGHEST


def with_halo(cells, sides, width):
    for axis, dim in sides:
        count = lax.axis_size(axis)
        ends = count - 1
        head = lax.slice_in_dim(cells, 0, width, axis=dim)
        tail = lax.slice_in_dim(cells, cells.shape[dim] - width, cells.shape[dim], axis=dim)
        cells = jnp.concatenate(
            [
                lax.ppermute(tail, axis, [(i, (i + 1) % count) for i in range(ends)]),
                cells,
                lax.ppermute(head, axis, [((i + 1) % count, i) for i in range(ends)]),
            ],
            axis=dim,
        )
    return cells


def sent_to_all(array, axis):
    size = lax.axis_size(axis)
    return lax.all_to_all(
        jnp.broadcast_to(array[None], (size, *array.shape)), axis, 0, 0, tiled=True
    )


def over_copies(array, axis):
    return sent_to_all(array, axis).sum(axis=0)


def together(arrays, axis):
    vector, at, outs = (jnp.concatenate([a.reshape(-1) for a in arrays]), 0, [])
    running = over_copies(vector, axis)
    for a in arrays:
        outs.append(running[at : at + a.size].reshape(a.shape))
        at += a.size
    return tuple(outs)


def in_order(tiles, dim):
    dims = list(tiles.shape[1:])
    dims[dim] *= tiles.shape[0]
    return jnp.moveaxis(tiles, 0, dim).reshape(dims)


def collect_2(array, axis, dim):
    tiles = sent_to_all(array, axis)
    return in_order(tiles, dim)


def axis_smooth(values_in, axis_number):
    pads = [(1, 1) if position == axis_number else (0, 0) for position in range(values_in.ndim)]
    padded = jnp.pad(values_in, pads)
    extent = values_in.shape[axis_number]
    return (
        0.5 * lax.slice_in_dim(padded, 0, extent, axis=axis_number)
        + lax.slice_in_dim(padded, 1, extent + 1, axis=axis_number)
        + 0.5 * lax.slice_in_dim(padded, 2, extent + 2, axis=axis_number)
    )


def operator_apply(vectors, density_cells, plane_mask, density_wide):
    masked = vectors * plane_mask
    extent = masked.shape[1]
    masked_wide = with_halo(masked, (("halo", 1),), 1)
    padded = jnp.stack([masked_wide, masked_wide * density_wide[None]])
    summed = (
        0.5 * padded[:, :, :extent]
        + padded[:, :, 1 : extent + 1]
        + 0.5 * padded[:, :, 2 : extent + 2]
    )
    summed = axis_smooth(summed, 3)
    summed = axis_smooth(summed, 4)
    return plane_mask * (density_cells * summed[0] + summed[1]) / 16.0


def gram_local(left_rows, right_rows):
    return jnp.einsum("kp,jp->kj", left_rows, right_rows, precision=EXACT)


def reduce_solve(
    own_reduced,
    other_reduced,
    own_rows,
    other_rows,
    stiff_all,
    own_first,
    start_block,
    coupling_scale,
):
    first_reduced = jnp.where(own_first, own_reduced, other_reduced)
    second_reduced = jnp.where(own_first, other_reduced, own_reduced)
    first_rows = coupling_scale * jnp.where(own_first, own_rows, other_rows)
    second_rows = coupling_scale * jnp.where(own_first, other_rows, own_rows)
    zero_block = jnp.zeros_like(first_reduced)
    matrix = jnp.block(
        [
            [first_reduced, zero_block, first_rows.T],
            [zero_block, second_reduced, second_rows.T],
            [first_rows, second_rows, jnp.diag(stiff_all)],
        ]
    )
    coeffs = start_block
    for inner_step in range(RITERS):
        product = jnp.dot(matrix, coeffs, precision=EXACT)
        gram_small = jnp.dot(product.T, product, precision=EXACT)
        lower_factor = jnp.linalg.cholesky(gram_small)
        coeffs = jax.scipy.linalg.solve_triangular(lower_factor, product.T, lower=True).T
    reduced_next = jnp.dot(coeffs.T, jnp.dot(matrix, coeffs, precision=EXACT), precision=EXACT)
    return (coeffs, reduced_next)


def per_device(start_modes, density, planes, tree_order, iface_index, iface_stiff, reduced_start):
    keep_modes = start_modes.shape[1]
    block_shape = start_modes.shape[1:]
    local_cells = start_modes.shape[2] * start_modes.shape[3] * start_modes.shape[4]
    halo_size = lax.axis_size("halo")
    leaf_size = lax.axis_size("leaf")
    halo_index = lax.axis_index("halo")
    leaf_index = lax.axis_index("leaf")
    iface_local = iface_index.shape[2]
    total_cells = local_cells * halo_size
    plane_ids = halo_index * start_modes.shape[2] + jnp.arange(
        start_modes.shape[2], dtype=jnp.int32
    )
    plane_mask = (plane_ids < planes[0]).astype(jnp.float32)[:, None, None]
    density_cells = density[0]
    density_wide = with_halo(density_cells, (("halo", 0),), 1)
    vectors = start_modes[0].astype(jnp.float32)
    vectors = operator_apply(vectors, density_cells, plane_mask, density_wide)
    image_block = operator_apply(vectors, density_cells, plane_mask, density_wide)
    image_rows = image_block.reshape(keep_modes, local_cells)
    applied = operator_apply(image_block, density_cells, plane_mask, density_wide).reshape(
        keep_modes, local_cells
    )
    gram_total, cross_total = together(
        (gram_local(image_rows, image_rows), gram_local(image_rows, applied)), "halo"
    )
    lower_factor = jnp.linalg.cholesky(gram_total)
    basis_rows = jax.scipy.linalg.solve_triangular(lower_factor, image_rows, lower=True)
    half_step = jax.scipy.linalg.solve_triangular(lower_factor, cross_total, lower=True)
    reduced_own = jax.scipy.linalg.solve_triangular(lower_factor, half_step.T, lower=True).T
    leaf_ids = jnp.arange(leaf_size, dtype=jnp.int32)
    cell_ids = jnp.arange(local_cells, dtype=jnp.int32)
    own_position = tree_order[leaf_index]
    coupling_scale = 0.5 * math.sqrt(total_cells / keep_modes)
    rows_share = keep_modes // halo_size
    for level_index in range(LEVELS):
        group_step = 2**level_index
        own_block = own_position // group_step
        other_block = jnp.bitwise_xor(own_block, 1)
        blocks_all = tree_order // group_step
        own_least = jnp.min(jnp.where(blocks_all == own_block, leaf_ids, leaf_size))
        other_least = jnp.min(jnp.where(blocks_all == other_block, leaf_ids, leaf_size))
        own_first = own_least < other_least
        positions = iface_index[0, level_index]
        stiffness = iface_stiff[0, level_index]
        own_rows = jnp.take(basis_rows, positions, axis=1).T
        rows_zero = jnp.zeros((iface_local, keep_modes), jnp.float32)
        stiff_zero = jnp.zeros((iface_local,), jnp.float32)
        slice_rows = lax.dynamic_slice_in_dim(reduced_own, halo_index * rows_share, rows_share, 0)
        initial = (
            jnp.zeros((rows_share, keep_modes), jnp.float32),
            rows_zero,
            rows_zero,
            stiff_zero,
        )
        reduced_piece = collect_2(slice_rows[None], "leaf", 0)
        rows_piece = collect_2(own_rows[None], "leaf", 0)
        stiff_piece = collect_2(stiffness[None], "leaf", 0)
        piece_ids = jnp.arange(reduced_piece.shape[0], dtype=jnp.int32)
        piece_position = jnp.take(tree_order, piece_ids)
        piece_blocks = piece_position // group_step
        same_weight = ((piece_blocks == own_block) & (piece_ids != leaf_index)).astype(jnp.float32)
        other_weight = (piece_blocks == other_block).astype(jnp.float32)
        rep_weight = (piece_position == other_block * group_step).astype(jnp.float32)
        other_slice = initial[0] + jnp.einsum(
            "n,nij->ij", rep_weight, reduced_piece, precision=EXACT
        )
        same_rows = initial[1] + jnp.einsum("n,nij->ij", same_weight, rows_piece, precision=EXACT)
        other_rows = initial[2] + jnp.einsum("n,nij->ij", other_weight, rows_piece, precision=EXACT)
        rest_stiff = jnp.einsum("n,ni->i", same_weight + other_weight, stiff_piece, precision=EXACT)
        pair_rows, stiff_all, other_reduced = (
            collect_2(jnp.stack([own_rows + same_rows, other_rows]), "halo", 1),
            collect_2(stiffness + rest_stiff, "halo", 0),
            collect_2(other_slice, "halo", 0),
        )
        coeffs, reduced_next = reduce_solve(
            reduced_own,
            other_reduced,
            pair_rows[0],
            pair_rows[1],
            stiff_all,
            own_first,
            reduced_start,
            coupling_scale,
        )
        own_coeffs = jnp.where(own_first, coeffs[:keep_modes], coeffs[keep_modes : 2 * keep_modes])
        iface_coeffs = lax.dynamic_slice_in_dim(
            coeffs, 2 * keep_modes + halo_index * iface_local, iface_local, 0
        )
        indicator = (positions[:, None] == cell_ids[None, :]).astype(jnp.float32)
        weight_factor = 1.0 / math.sqrt(2 ** (level_index + 1))
        basis_rows = jnp.einsum(
            "kj,kp->jp", own_coeffs, basis_rows, precision=EXACT
        ) + weight_factor * jnp.einsum("ij,ip->jp", iface_coeffs, indicator, precision=EXACT)
        reduced_own = reduced_next
    modes = (math.sqrt(total_cells) * basis_rows).reshape((1,) + tuple(block_shape))
    return (modes, reduced_own[None])


def solution(mesh):
    return jax.shard_map(
        per_device,
        mesh=mesh,
        in_specs=(
            P("leaf", None, "halo", None, None),
            P("leaf", "halo", None, None),
            P("leaf"),
            P(),
            P("leaf", None, "halo"),
            P("leaf", None, "halo"),
            P(),
        ),
        out_specs=(P("leaf", None, "halo", None, None), P("leaf", None, None)),
        check_vma=False,
    )
```

profile of v0, /device:TPU:1, one launch (start us, length us, event | category | flops | bytes accessed | tf_op | source)
XLA Modules:
  0.0 402.7 jit_solution(12824382553458928090)
XLA Ops:
  2.8 8.7 %collective-permute-start.1 = (f32[128,1,4,128]{3,2,1,0:T(4,128)S(1)}, f32[128,1,4,128]{3,2,1,0:T(4,128)S(1)}, u32[]{:S(2)}, u32[]{:S(2)}) collective-permute-start(f32[128,1,4,128]{3,2,1,0:T(4,128)S(1)} %get-tuple-element.24), channel_id=1, source_target_pairs={{64,0},{128,64},{192,128},{256,192},{320,256},{384,320},{448,384},... | collective-permute-start | bytes 786440 | tf_op jit(solution)/shard_map/ppermute | solution.py:25
  11.6 1.9 collective-permute-start
  13.5 2.4 collective-permute-start.3
  15.9 3.1 collective-permute-start.2
  19.8 12.1 %all-to-all-start.5 = ((f32[64,1,16]{2,1,0:T(1,128)}), f32[64,1,16]{2,1,0:T(1,128)S(1)}, u32[]{:S(2)}, u32[]{:S(2)}) async-start(f32[64,1,16]{2,1,0:T(1,128)} %broadcast_in_dim.136), calls=%async_computation.5 | async-start | bytes 65536 | tf_op jit(solution)/shard_map/all_to_all | solution.py:34
  35.3 2.2 fusion.20
  38.0 1.9 collective-permute-start.5
  39.9 4.2 %collective-permute-start.4 = (f32[128,1,4,128]{3,2,1,0:T(4,128)S(1)}, f32[128,1,4,128]{3,2,1,0:T(4,128)S(1)}, u32[]{:S(2)}, u32[]{:S(2)}) collective-permute-start(f32[128,1,4,128]{3,2,1,0:T(4,128)S(1)} %get-tuple-element.21), channel_id=1, source_target_pairs={{0,64},{64,128},{128,192},{192,256},{256,320},{320,384},{384,448},... | collective-permute-start | bytes 786440 | tf_op jit(solution)/shard_map/ppermute | solution.py:23
  50.1 2.2 fusion.24
  53.2 1.9 collective-permute-start.7
  55.1 4.6 %collective-permute-start.6 = (f32[128,1,4,128]{3,2,0,1:T(4,128)S(1)}, f32[128,1,4,128]{3,2,0,1:T(4,128)S(1)}, u32[]{:S(2)}, u32[]{:S(2)}) collective-permute-start(f32[128,1,4,128]{3,2,0,1:T(4,128)S(1)} %get-tuple-element.19), channel_id=1, source_target_pairs={{0,64},{64,128},{128,192},{192,256},{256,320},{320,384},{384,448},... | collective-permute-start | bytes 786440 | tf_op jit(solution)/shard_map/ppermute | solution.py:23
  59.7 1.5 convolution_bitcast_fusion.1
  66.0 2.2 fusion.28
  68.6 1.5 convolution_bitcast_fusion
  70.2 1.5 broadcast_in_dim.131
  71.7 5.7 %all-to-all-start = ((f32[8,1,32768]{2,1,0:T(1,128)}), f32[8,1,32768]{2,1,0:T(1,128)S(1)}, u32[]{:S(2)}, u32[]{:S(2)}) async-start(f32[8,1,32768]{2,1,0:T(1,128)} %broadcast_in_dim.131), calls=%async_computation | async-start | bytes 2097152 | tf_op jit(solution)/shard_map/all_to_all | solution.py:34
  84.3 8.1 %all-to-all-done = f32[8,1,32768]{2,1,0:T(1,128)S(1)} async-done(((f32[8,1,32768]{2,1,0:T(1,128)}), f32[8,1,32768]{2,1,0:T(1,128)S(1)}, u32[]{:S(2)}, u32[]{:S(2)}) %all-to-all-start) | async-done | bytes 1048608 | tf_op jit(solution)/shard_map/all_to_all | solution.py:34
  93.0 12.6 %all-to-all-start.11 = ((f32[64,1,16]{2,1,0:T(1,128)}), f32[64,1,16]{2,1,0:T(1,128)}, u32[]{:S(2)}, u32[]{:S(2)}) async-start(f32[64,1,16]{2,1,0:T(1,128)} %broadcast_in_dim.144), calls=%async_computation.11 | async-start | bytes 65536 | tf_op jit(solution)/shard_map/all_to_all | solution.py:34
  106.5 11.7 %cholesky.89 = f32[128,128]{1,0:T(8,128)S(1)} custom-call(f32[128,128]{1,0:T(8,128)S(1)} %fusion.108), custom_call_target="Cholesky" | custom-call | tf_op jit(solution)/shard_map/jit(cholesky)/cholesky | solution.py:151
  119.6 9.8 %custom-call.18 = f32[1,128,128]{1,2,0:T(8,128)S(1)} custom-call(f32[1,128,128]{2,1,0:T(8,128)S(1)} %fusion.86), custom_call_target="InvertDiagBlocksLowerTriangular" | custom-call | tf_op jit(solution)/shard_map/jit(_solve_triangular)/triangular_solve | solution.py:154
  132.0 4.5 %all-to-all-start.6 = ((f32[8,1,16]{2,1,0:T(1,128)}), f32[8,1,16]{2,1,0:T(1,128)S(1)}, u32[]{:S(2)}, u32[]{:S(2)}) async-start(f32[8,1,16]{2,1,0:T(1,128)} %broadcast_in_dim.137), calls=%async_computation.6 | async-start | bytes 8192 | tf_op jit(solution)/shard_map/all_to_all | solution.py:34
  136.5 4.5 %all-to-all-done.6 = f32[8,1,16]{2,1,0:T(1,128)S(1)} async-done(((f32[8,1,16]{2,1,0:T(1,128)}), f32[8,1,16]{2,1,0:T(1,128)S(1)}, u32[]{:S(2)}, u32[]{:S(2)}) %all-to-all-start.6) | async-done | bytes 544 | tf_op jit(solution)/shard_map/all_to_all | solution.py:34
  141.8 12.5 %all-to-all-start.3 = ((f32[64,1,16,128]{3,2,1,0:T(8,128)}), f32[64,1,16,128]{3,2,1,0:T(8,128)S(1)}, u32[]{:S(2)}, u32[]{:S(2)}) async-start(f32[64,1,16,128]{3,2,1,0:T(8,128)} %broadcast_in_dim.134), calls=%async_computation.3 | async-start | bytes 1048576 | tf_op jit(solution)/shard_map/all_to_all | solution.py:34
  157.5 13.3 %all-to-all-done.3 = f32[64,1,16,128]{3,2,1,0:T(8,128)S(1)} async-done(((f32[64,1,16,128]{3,2,1,0:T(8,128)}), f32[64,1,16,128]{3,2,1,0:T(8,128)S(1)}, u32[]{:S(2)}, u32[]{:S(2)}) %all-to-all-start.3) | async-done | bytes 524320 | tf_op jit(solution)/shard_map/all_to_all | solution.py:34
  171.6 7.8 %all-to-all-start.1 = ((f32[64,1,16,128]{3,2,1,0:T(8,128)}), f32[64,1,16,128]{3,2,1,0:T(8,128)S(1)}, u32[]{:S(2)}, u32[]{:S(2)}) async-start(f32[64,1,16,128]{3,2,1,0:T(8,128)} %broadcast_in_dim.132), calls=%async_computation.1 | async-start | bytes 1048576 | tf_op jit(solution)/shard_map/all_to_all | solution.py:34
  183.2 12.5 %all-to-all-done.1 = f32[64,1,16,128]{3,2,1,0:T(8,128)S(1)} async-done(((f32[64,1,16,128]{3,2,1,0:T(8,128)}), f32[64,1,16,128]{3,2,1,0:T(8,128)S(1)}, u32[]{:S(2)}, u32[]{:S(2)}) %all-to-all-start.1) | async-done | bytes 524320 | tf_op jit(solution)/shard_map/all_to_all | solution.py:34
  196.8 7.1 %all-to-all-start.2 = ((f32[8,16,128]{2,1,0:T(8,128)}), f32[8,16,128]{2,1,0:T(8,128)S(1)}, u32[]{:S(2)}, u32[]{:S(2)}) async-start(f32[8,16,128]{2,1,0:T(8,128)} %broadcast_in_dim.133), calls=%async_computation.2 | async-start | bytes 131072 | tf_op jit(solution)/shard_map/all_to_all | solution.py:34
  203.9 4.9 %all-to-all-done.2 = f32[8,16,128]{2,1,0:T(8,128)S(1)} async-done(((f32[8,16,128]{2,1,0:T(8,128)}), f32[8,16,128]{2,1,0:T(8,128)S(1)}, u32[]{:S(2)}, u32[]{:S(2)}) %all-to-all-start.2) | async-done | bytes 65568 | tf_op jit(solution)/shard_map/all_to_all | solution.py:34
  209.5 4.1 %all-to-all-start.4 = ((f32[8,2,16,128]{3,2,1,0:T(8,128)}), f32[8,2,16,128]{3,2,1,0:T(8,128)S(1)}, u32[]{:S(2)}, u32[]{:S(2)}) async-start(f32[8,2,16,128]{3,2,1,0:T(8,128)} %broadcast_in_dim.135), calls=%async_computation.4 | async-start | bytes 262144 | tf_op jit(solution)/shard_map/all_to_all | solution.py:34
  213.5 5.3 %all-to-all-done.4 = f32[8,2,16,128]{3,2,1,0:T(8,128)S(1)} async-done(((f32[8,2,16,128]{3,2,1,0:T(8,128)}), f32[8,2,16,128]{3,2,1,0:T(8,128)S(1)}, u32[]{:S(2)}, u32[]{:S(2)}) %all-to-all-start.4) | async-done | bytes 131104 | tf_op jit(solution)/shard_map/all_to_all | solution.py:34
  219.4 4.5 %all-to-all-start.12 = ((f32[8,1,16]{2,1,0:T(1,128)}), f32[8,1,16]{2,1,0:T(1,128)S(1)}, u32[]{:S(2)}, u32[]{:S(2)}) async-start(f32[8,1,16]{2,1,0:T(1,128)} %broadcast_in_dim.145), calls=%async_computation.12 | async-start | bytes 8192 | tf_op jit(solution)/shard_map/all_to_all | solution.py:34
  225.4 11.7 %cholesky.100 = f32[128,128]{1,0:T(8,128)S(1)} custom-call(f32[128,128]{1,0:T(8,128)S(1)} %fusion.102), custom_call_target="Cholesky" | custom-call | tf_op jit(solution)/shard_map/jit(cholesky)/cholesky | solution.py:119
  238.4 9.8 %custom-call.19 = f32[1,128,128]{1,2,0:T(8,128)S(1)} custom-call(f32[1,128,128]{2,1,0:T(8,128)S(1)} %fusion.87), custom_call_target="InvertDiagBlocksLowerTriangular" | custom-call | tf_op jit(solution)/shard_map/jit(_solve_triangular)/triangular_solve | solution.py:120
  249.9 11.9 %cholesky.111 = f32[128,128]{1,0:T(8,128)S(1)} custom-call(f32[128,128]{1,0:T(8,128)S(1)} %fusion.100), custom_call_target="Cholesky" | custom-call | tf_op jit(solution)/shard_map/jit(cholesky)/cholesky | solution.py:119
  263.1 9.8 %custom-call.20 = f32[1,128,128]{1,2,0:T(8,128)S(1)} custom-call(f32[1,128,128]{2,1,0:T(8,128)S(1)} %fusion.88), custom_call_target="InvertDiagBlocksLowerTriangular" | custom-call | tf_op jit(solution)/shard_map/jit(_solve_triangular)/triangular_solve | solution.py:120
  277.0 5.1 %all-to-all-start.9 = ((f32[64,1,16,128]{3,2,1,0:T(8,128)}), f32[64,1,16,128]{3,2,1,0:T(8,128)S(1)}, u32[]{:S(2)}, u32[]{:S(2)}) async-start(f32[64,1,16,128]{3,2,1,0:T(8,128)} %broadcast_in_dim.142), calls=%async_computation.9 | async-start | bytes 1048576 | tf_op jit(solution)/shard_map/all_to_all | solution.py:34
  283.1 16.3 %all-to-all-done.9 = f32[64,1,16,128]{3,2,1,0:T(8,128)S(1)} async-done(((f32[64,1,16,128]{3,2,1,0:T(8,128)}), f32[64,1,16,128]{3,2,1,0:T(8,128)S(1)}, u32[]{:S(2)}, u32[]{:S(2)}) %all-to-all-start.9) | async-done | bytes 524320 | tf_op jit(solution)/shard_map/all_to_all | solution.py:34
  300.2 7.2 %all-to-all-start.7 = ((f32[64,1,16,128]{3,2,1,0:T(8,128)}), f32[64,1,16,128]{3,2,1,0:T(8,128)S(1)}, u32[]{:S(2)}, u32[]{:S(2)}) async-start(f32[64,1,16,128]{3,2,1,0:T(8,128)} %broadcast_in_dim.140), calls=%async_computation.7 | async-start | bytes 1048576 | tf_op jit(solution)/shard_map/all_to_all | solution.py:34
  311.1 12.6 %all-to-all-done.7 = f32[64,1,16,128]{3,2,1,0:T(8,128)S(1)} async-done(((f32[64,1,16,128]{3,2,1,0:T(8,128)}), f32[64,1,16,128]{3,2,1,0:T(8,128)S(1)}, u32[]{:S(2)}, u32[]{:S(2)}) %all-to-all-start.7) | async-done | bytes 524320 | tf_op jit(solution)/shard_map/all_to_all | solution.py:34
  324.8 8.1 %all-to-all-start.8 = ((f32[8,16,128]{2,1,0:T(8,128)}), f32[8,16,128]{2,1,0:T(8,128)S(1)}, u32[]{:S(2)}, u32[]{:S(2)}) async-start(f32[8,16,128]{2,1,0:T(8,128)} %broadcast_in_dim.141), calls=%async_computation.8 | async-start | bytes 131072 | tf_op jit(solution)/shard_map/all_to_all | solution.py:34
  332.9 4.8 %all-to-all-done.8 = f32[8,16,128]{2,1,0:T(8,128)S(1)} async-done(((f32[8,16,128]{2,1,0:T(8,128)}), f32[8,16,128]{2,1,0:T(8,128)S(1)}, u32[]{:S(2)}, u32[]{:S(2)}) %all-to-all-start.8) | async-done | bytes 65568 | tf_op jit(solution)/shard_map/all_to_all | solution.py:34
  338.4 4.2 %all-to-all-start.10 = ((f32[8,2,16,128]{3,2,1,0:T(8,128)}), f32[8,2,16,128]{3,2,1,0:T(8,128)S(1)}, u32[]{:S(2)}, u32[]{:S(2)}) async-start(f32[8,2,16,128]{3,2,1,0:T(8,128)} %broadcast_in_dim.143), calls=%async_computation.10 | async-start | bytes 262144 | tf_op jit(solution)/shard_map/all_to_all | solution.py:34
  342.7 5.0 %all-to-all-done.10 = f32[8,2,16,128]{3,2,1,0:T(8,128)S(1)} async-done(((f32[8,2,16,128]{3,2,1,0:T(8,128)}), f32[8,2,16,128]{3,2,1,0:T(8,128)S(1)}, u32[]{:S(2)}, u32[]{:S(2)}) %all-to-all-start.10) | async-done | bytes 131104 | tf_op jit(solution)/shard_map/all_to_all | solution.py:34
  349.2 11.7 %cholesky.122 = f32[128,128]{1,0:T(8,128)S(1)} custom-call(f32[128,128]{1,0:T(8,128)S(1)} %fusion.98), custom_call_target="Cholesky" | custom-call | tf_op jit(solution)/shard_map/jit(cholesky)/cholesky | solution.py:119
  362.3 9.8 %custom-call.21 = f32[1,128,128]{1,2,0:T(8,128)S(1)} custom-call(f32[1,128,128]{2,1,0:T(8,128)S(1)} %fusion.89), custom_call_target="InvertDiagBlocksLowerTriangular" | custom-call | tf_op jit(solution)/shard_map/jit(_solve_triangular)/triangular_solve | solution.py:120
  373.7 11.9 %cholesky.133 = f32[128,128]{1,0:T(8,128)S(1)} custom-call(f32[128,128]{1,0:T(8,128)S(1)} %fusion.96), custom_call_target="Cholesky" | custom-call | tf_op jit(solution)/shard_map/jit(cholesky)/cholesky | solution.py:119
  387.0 9.8 %custom-call.22 = f32[1,128,128]{1,2,0:T(8,128)S(1)} custom-call(f32[1,128,128]{2,1,0:T(8,128)S(1)} %fusion.90), custom_call_target="InvertDiagBlocksLowerTriangular" | custom-call | tf_op jit(solution)/shard_map/jit(_solve_triangular)/triangular_solve | solution.py:120
  399.8 1.7 reshape.316
  (175 shorter events, 61.9 us)
Async XLA Ops:
  0.6 223.5 %copy-start = (f32[384,128]{1,0:T(8,128)S(1)}, f32[384,128]{1,0:T(8,128)}, u32[]{:S(2)}) copy-start(f32[384,128]{1,0:T(8,128)} %param.22) | copy-start | bytes 589828
  0.6 31.2 %copy-start.2 = (bf16[1,128,4,4,128]{4,3,2,1,0:T(4,128)(2,1)S(1)}, bf16[1,128,4,4,128]{4,3,2,1,0:T(4,128)(2,1)}, u32[]{:S(2)}) copy-start(bf16[1,128,4,4,128]{4,3,2,1,0:T(4,128)(2,1)} %param.16) | copy-start | bytes 1572868
  0.7 12.8 %copy-start.3 = (f32[1,4,4,128]{3,2,1,0:T(4,128)S(1)}, f32[1,4,4,128]{3,2,1,0:T(4,128)}, u32[]{:S(2)}) copy-start(f32[1,4,4,128]{3,2,1,0:T(4,128)} %param.17) | copy-start | bytes 24580
  0.7 18.4 %copy-start.4 = (f32[1,2,16]{2,1,0:T(2,128)S(1)}, f32[1,2,16]{2,1,0:T(2,128)}, u32[]{:S(2)}) copy-start(f32[1,2,16]{2,1,0:T(2,128)} %param.21) | copy-start | bytes 388
  2.8 29.3 %collective-permute-start.1 = (f32[128,1,4,128]{3,2,1,0:T(4,128)S(1)}, f32[128,1,4,128]{3,2,1,0:T(4,128)S(1)}, u32[]{:S(2)}, u32[]{:S(2)}) collective-permute-start(f32[128,1,4,128]{3,2,1,0:T(4,128)S(1)} %get-tuple-element.24), channel_id=1, source_target_pairs={{64,0},{128,64},{192,128},{256,192},{320,256},{384,320},{448,384},... | collective-permute-start | bytes 786440 | tf_op jit(solution)/shard_map/ppermute | solution.py:25
  11.6 20.6 %collective-permute-start = (f32[128,1,4,128]{3,2,1,0:T(4,128)S(1)}, f32[128,1,4,128]{3,2,1,0:T(4,128)S(1)}, u32[]{:S(2)}, u32[]{:S(2)}) collective-permute-start(f32[128,1,4,128]{3,2,1,0:T(4,128)S(1)} %get-tuple-element.23), channel_id=1, source_target_pairs={{0,64},{64,128},{128,192},{192,256},{256,320},{320,384},{384,448},... | collective-permute-start | bytes 786440 | tf_op jit(solution)/shard_map/ppermute | solution.py:23
  13.5 18.6 %collective-permute-start.3 = (f32[1,4,128]{2,1,0:T(4,128)S(1)}, f32[1,4,128]{2,1,0:T(4,128)S(1)}, u32[]{:S(2)}, u32[]{:S(2)}) collective-permute-start(f32[1,4,128]{2,1,0:T(4,128)S(1)} %get-tuple-element.34), channel_id=1, source_target_pairs={{64,0},{128,64},{192,128},{256,192},{320,256},{384,320},{448,384},... | collective-permute-start | bytes 6152 | tf_op jit(solution)/shard_map/ppermute | solution.py:25
  15.9 16.2 %collective-permute-start.2 = (f32[1,4,128]{2,1,0:T(4,128)S(1)}, f32[1,4,128]{2,1,0:T(4,128)S(1)}, u32[]{:S(2)}, u32[]{:S(2)}) collective-permute-start(f32[1,4,128]{2,1,0:T(4,128)S(1)} %get-tuple-element.33), channel_id=1, source_target_pairs={{0,64},{64,128},{128,192},{192,256},{256,320},{320,384},{384,448},... | collective-permute-start | bytes 6152 | tf_op jit(solution)/shard_map/ppermute | solution.py:23
  19.8 50.4 %all-to-all-start.5 = ((f32[64,1,16]{2,1,0:T(1,128)}), f32[64,1,16]{2,1,0:T(1,128)S(1)}, u32[]{:S(2)}, u32[]{:S(2)}) async-start(f32[64,1,16]{2,1,0:T(1,128)} %broadcast_in_dim.136), calls=%async_computation.5 | async-start | bytes 65536 | tf_op jit(solution)/shard_map/all_to_all | solution.py:34
  38.0 7.7 %collective-permute-start.5 = (f32[128,1,4,128]{3,2,1,0:T(4,128)S(1)}, f32[128,1,4,128]{3,2,1,0:T(4,128)S(1)}, u32[]{:S(2)}, u32[]{:S(2)}) collective-permute-start(f32[128,1,4,128]{3,2,1,0:T(4,128)S(1)} %get-tuple-element.22), channel_id=1, source_target_pairs={{64,0},{128,64},{192,128},{256,192},{320,256},{384,320},{448,384},... | collective-permute-start | bytes 786440 | tf_op jit(solution)/shard_map/ppermute | solution.py:25
  39.9 6.9 %collective-permute-start.4 = (f32[128,1,4,128]{3,2,1,0:T(4,128)S(1)}, f32[128,1,4,128]{3,2,1,0:T(4,128)S(1)}, u32[]{:S(2)}, u32[]{:S(2)}) collective-permute-start(f32[128,1,4,128]{3,2,1,0:T(4,128)S(1)} %get-tuple-element.21), channel_id=1, source_target_pairs={{0,64},{64,128},{128,192},{192,256},{256,320},{320,384},{384,448},... | collective-permute-start | bytes 786440 | tf_op jit(solution)/shard_map/ppermute | solution.py:23
  53.2 8.4 %collective-permute-start.7 = (f32[128,1,4,128]{3,2,0,1:T(4,128)S(1)}, f32[128,1,4,128]{3,2,0,1:T(4,128)S(1)}, u32[]{:S(2)}, u32[]{:S(2)}) collective-permute-start(f32[128,1,4,128]{3,2,0,1:T(4,128)S(1)} %get-tuple-element.20), channel_id=1, source_target_pairs={{64,0},{128,64},{192,128},{256,192},{320,256},{384,320},{448,384},... | collective-permute-start | bytes 786440 | tf_op jit(solution)/shard_map/ppermute | solution.py:25
  55.1 7.7 %collective-permute-start.6 = (f32[128,1,4,128]{3,2,0,1:T(4,128)S(1)}, f32[128,1,4,128]{3,2,0,1:T(4,128)S(1)}, u32[]{:S(2)}, u32[]{:S(2)}) collective-permute-start(f32[128,1,4,128]{3,2,0,1:T(4,128)S(1)} %get-tuple-element.19), channel_id=1, source_target_pairs={{0,64},{64,128},{128,192},{192,256},{256,320},{320,384},{384,448},... | collective-permute-start | bytes 786440 | tf_op jit(solution)/shard_map/ppermute | solution.py:23
  70.1 7.2 %copy-start.1 = (s32[64]{0:T(128)S(1)}, s32[64]{0:T(128)}, u32[]{:S(2)}) copy-start(s32[64]{0:T(128)} %param.19) | copy-start | bytes 772
  70.1 11.8 %copy-start.7 = (s32[1,2,16]{2,1,0:T(2,128)S(1)}, s32[1,2,16]{2,1,0:T(2,128)}, u32[]{:S(2)}) copy-start(s32[1,2,16]{2,1,0:T(2,128)} %param.20) | copy-start | bytes 388
  71.7 20.6 %all-to-all-start = ((f32[8,1,32768]{2,1,0:T(1,128)}), f32[8,1,32768]{2,1,0:T(1,128)S(1)}, u32[]{:S(2)}, u32[]{:S(2)}) async-start(f32[8,1,32768]{2,1,0:T(1,128)} %broadcast_in_dim.131), calls=%async_computation | async-start | bytes 2097152 | tf_op jit(solution)/shard_map/all_to_all | solution.py:34
  93.0 38.4 %all-to-all-start.11 = ((f32[64,1,16]{2,1,0:T(1,128)}), f32[64,1,16]{2,1,0:T(1,128)}, u32[]{:S(2)}, u32[]{:S(2)}) async-start(f32[64,1,16]{2,1,0:T(1,128)} %broadcast_in_dim.144), calls=%async_computation.11 | async-start | bytes 65536 | tf_op jit(solution)/shard_map/all_to_all | solution.py:34
  130.4 1.0 copy-start.9
  130.4 6.0 %copy-start.6 = (pred[16]{0:T(512)(128)(4,1)S(1)}, pred[16]{0:T(512)(128)(4,1)}, u32[]{:S(2)}) copy-start(pred[16]{0:T(512)(128)(4,1)} %get-tuple-element.37) | copy-start | bytes 52
  130.5 26.5 %copy-start.10 = (s32[16]{0:T(128)S(1)}, s32[16]{0:T(128)}, u32[]{:S(2)}) copy-start(s32[16]{0:T(128)} %get-tuple-element.12) | copy-start | bytes 196
  130.5 26.5 %copy-start.8 = (s32[1,2,16]{2,1,0:T(2,128)S(1)}, s32[1,2,16]{2,1,0:T(2,128)}, u32[]{:S(2)}) copy-start(s32[1,2,16]{2,1,0:T(2,128)} %param.20) | copy-start | bytes 388
  132.0 9.0 %all-to-all-start.6 = ((f32[8,1,16]{2,1,0:T(1,128)}), f32[8,1,16]{2,1,0:T(1,128)S(1)}, u32[]{:S(2)}, u32[]{:S(2)}) async-start(f32[8,1,16]{2,1,0:T(1,128)} %broadcast_in_dim.137), calls=%async_computation.6 | async-start | bytes 8192 | tf_op jit(solution)/shard_map/all_to_all | solution.py:34
  141.8 29.0 %all-to-all-start.3 = ((f32[64,1,16,128]{3,2,1,0:T(8,128)}), f32[64,1,16,128]{3,2,1,0:T(8,128)S(1)}, u32[]{:S(2)}, u32[]{:S(2)}) async-start(f32[64,1,16,128]{3,2,1,0:T(8,128)} %broadcast_in_dim.134), calls=%async_computation.3 | async-start | bytes 1048576 | tf_op jit(solution)/shard_map/all_to_all | solution.py:34
  171.6 24.1 %all-to-all-start.1 = ((f32[64,1,16,128]{3,2,1,0:T(8,128)}), f32[64,1,16,128]{3,2,1,0:T(8,128)S(1)}, u32[]{:S(2)}, u32[]{:S(2)}) async-start(f32[64,1,16,128]{3,2,1,0:T(8,128)} %broadcast_in_dim.132), calls=%async_computation.1 | async-start | bytes 1048576 | tf_op jit(solution)/shard_map/all_to_all | solution.py:34
  196.8 12.0 %all-to-all-start.2 = ((f32[8,16,128]{2,1,0:T(8,128)}), f32[8,16,128]{2,1,0:T(8,128)S(1)}, u32[]{:S(2)}, u32[]{:S(2)}) async-start(f32[8,16,128]{2,1,0:T(8,128)} %broadcast_in_dim.133), calls=%async_computation.2 | async-start | bytes 131072 | tf_op jit(solution)/shard_map/all_to_all | solution.py:34
  209.5 9.3 %all-to-all-start.4 = ((f32[8,2,16,128]{3,2,1,0:T(8,128)}), f32[8,2,16,128]{3,2,1,0:T(8,128)S(1)}, u32[]{:S(2)}, u32[]{:S(2)}) async-start(f32[8,2,16,128]{3,2,1,0:T(8,128)} %broadcast_in_dim.135), calls=%async_computation.4 | async-start | bytes 262144 | tf_op jit(solution)/shard_map/all_to_all | solution.py:34
  219.4 56.8 %all-to-all-start.12 = ((f32[8,1,16]{2,1,0:T(1,128)}), f32[8,1,16]{2,1,0:T(1,128)S(1)}, u32[]{:S(2)}, u32[]{:S(2)}) async-start(f32[8,1,16]{2,1,0:T(1,128)} %broadcast_in_dim.145), calls=%async_computation.12 | async-start | bytes 8192 | tf_op jit(solution)/shard_map/all_to_all | solution.py:34
  274.5 1.6 copy-start.5
  277.0 22.3 %all-to-all-start.9 = ((f32[64,1,16,128]{3,2,1,0:T(8,128)}), f32[64,1,16,128]{3,2,1,0:T(8,128)S(1)}, u32[]{:S(2)}, u32[]{:S(2)}) async-start(f32[64,1,16,128]{3,2,1,0:T(8,128)} %broadcast_in_dim.142), calls=%async_computation.9 | async-start | bytes 1048576 | tf_op jit(solution)/shard_map/all_to_all | solution.py:34
  300.2 23.5 %all-to-all-start.7 = ((f32[64,1,16,128]{3,2,1,0:T(8,128)}), f32[64,1,16,128]{3,2,1,0:T(8,128)S(1)}, u32[]{:S(2)}, u32[]{:S(2)}) async-start(f32[64,1,16,128]{3,2,1,0:T(8,128)} %broadcast_in_dim.140), calls=%async_computation.7 | async-start | bytes 1048576 | tf_op jit(solution)/shard_map/all_to_all | solution.py:34
  324.8 13.0 %all-to-all-start.8 = ((f32[8,16,128]{2,1,0:T(8,128)}), f32[8,16,128]{2,1,0:T(8,128)S(1)}, u32[]{:S(2)}, u32[]{:S(2)}) async-start(f32[8,16,128]{2,1,0:T(8,128)} %broadcast_in_dim.141), calls=%async_computation.8 | async-start | bytes 131072 | tf_op jit(solution)/shard_map/all_to_all | solution.py:34
  338.4 9.3 %all-to-all-start.10 = ((f32[8,2,16,128]{3,2,1,0:T(8,128)}), f32[8,2,16,128]{3,2,1,0:T(8,128)S(1)}, u32[]{:S(2)}, u32[]{:S(2)}) async-start(f32[8,2,16,128]{3,2,1,0:T(8,128)} %broadcast_in_dim.143), calls=%async_computation.10 | async-start | bytes 262144 | tf_op jit(solution)/shard_map/all_to_all | solution.py:34
where the time goes:
time: 410 us; the launch traced here: 403 us
  other arithmetic  140 us (34%)
  starting transfers between devices  124 us (30%)
  waiting for transfers between devices  90.9 us (22%)
  matrix products  22 us (5%)
  local copies, waits for them, and re-layouts  17.4 us (4%)
  between operations  8.45 us (2%)
    all_to_all x13, starting transfers between devices, sent_to_all(): lax.all_to_all(jnp.broadcast_to(array[None], (size, *array.shape)), axis,...  95.4 us
    all_to_all x13, waiting for transfers between devices, sent_to_all(): lax.all_to_all(jnp.broadcast_to(array[None], (size, *array.shape)), axis,...  87.3 us
    another operation x12, other arithmetic, reduce_solve(): lower_factor = jnp.linalg.cholesky(gram_small)  49.9 us
    another operation x8, other arithmetic, reduce_solve(): jax.scipy.linalg.solve_triangular(lower_factor, product.T, lower=True)  41.9 us
    ppermute x4, starting transfers between devices, with_halo(): lax.ppermute(head, axis, [((i + 1) % count, i) for i in range(ends)])  15 us
    ppermute x4, starting transfers between devices, with_halo(): lax.ppermute(tail, axis, [(i, (i + 1) % count) for i in range(ends)])  13.8 us
    another operation x3, other arithmetic, per_device(): lower_factor = jnp.linalg.cholesky(gram_total)  12.4 us
    another operation x2, other arithmetic, per_device(): jax.scipy.linalg.solve_triangular(lower_factor, half_step.T, lower=True)  10.5 us
  transfers between devices with their start and end apart: 21, of which 14 were waited for; matrix products, arithmetic and copies ran while one was open for 28% of the time, Pallas kernels for 0%

commit v1 on v0

v1 whole, which is shorter than its diff:
```python
import math

import jax
import jax.numpy as jnp
from jax import lax
from jax.experimental import pallas as pl
from jax.experimental.pallas import tpu as pltpu
from jax.sharding import PartitionSpec as P

F32 = jnp.float32
HI = lax.Precision.HIGHEST
NV = 128
NC = 2048
SQ = 8
ROWS = 56
AG = 3 * ROWS + 40
VM = pl.BlockSpec(memory_space=pltpu.VMEM)
SM = pl.BlockSpec(memory_space=pltpu.SMEM)


def dot_nt(a, b):
    return lax.dot_general(a, b, (((1,), (1,)), ((), ())), precision=HI, preferred_element_type=F32)


def dot_nn(a, b):
    return lax.dot_general(a, b, (((1,), (0,)), ((), ())), precision=HI, preferred_element_type=F32)


def dot_tn(a, b):
    return lax.dot_general(a, b, (((0,), (0,)), ((), ())), precision=HI, preferred_element_type=F32)


def iota(shape, dim):
    return lax.broadcasted_iota(jnp.int32, shape, dim)


def shape(*dims):
    return jax.ShapeDtypeStruct(dims, F32)


def chol_inv(mats):
    count = len(mats)
    sh = (count, 8, NV)
    lane, sub = iota(sh, 2), iota(sh, 1)

    def over_lanes(x, c):
        return jnp.broadcast_to(x[:, :, c : c + 1], sh)

    def over_subs(x, r):
        return jnp.broadcast_to(x[:, r : r + 1, :], sh)

    rows = [jnp.stack([m[8 * i : 8 * i + 8, :] for m in mats]) for i in range(16)]
    for s in range(16):
        p = rows[s]
        cols = [over_lanes(p, 8 * s + j) for j in range(8)]
        scaled, scales, upper = [], [], {}
        for k in range(8):
            rs = lax.rsqrt(over_subs(cols[k], k))
            at = lane == 8 * s + k
            r = jnp.where(at, rs, over_subs(p, k) * rs)
            scaled.append(r)
            scales.append(rs)
            if k < 7:
                low = cols[k] * rs
                p = jnp.where(sub > k, jnp.where(at, 0.0, p) - low * r, p)
                for j in range(k + 1, 8):
                    upper[k, j] = over_subs(cols[j], k) * rs
                    cols[j] = cols[j] - low * upper[k, j]
        out = scaled[7]
        for k in range(7):
            out = jnp.where(sub == k, scaled[k], out)
        rows[s] = jnp.where(lane > 8 * s + sub, 0.0, out)
        inside = (lane >= 8 * s) & (lane < 8 * s + 8)
        kept = [jnp.where(inside & (lane > 8 * s + k), 0.0, scaled[k]) for k in range(8)]
        for a in range(s + 1, 16):
            q = rows[a]
            cols = [over_lanes(q, 8 * s + j) for j in range(8)]
            q = jnp.where(inside, 0.0, q)
            for k in range(8):
                low = cols[k] * scales[k]
                q = q - low * kept[k]
                for j in range(k + 1, 8):
                    cols[j] = cols[j] - low * upper[k, j]
            rows[a] = q
    return [jnp.concatenate([rows[i][b] for i in range(16)], axis=0) for b in range(count)]


def prep_kernel(planes, v, rho, left, right, wide):
    h = lax.axis_index("halo")
    wide[...] = v[...].astype(F32)
    for k in range(16):
        part = wide[pl.ds(k, NV, stride=16), :]
        part = jnp.where(h * 4 + k // 4 < planes[0], part, 0.0)
        if k < 12:
            left[k * NV : (k + 1) * NV, :] = part
        if k >= 4:
            right[(k - 4) * NV : (k - 3) * NV, :] = part
    left[12 * NV :, :] = rho[...]
    right[12 * NV : 12 * NV + 12, :] = rho[4:, :]
    right[12 * NV + 12 :, :] = rho[:4, :]


def smooth_first(cells):
    pairs = [[a + b for a, b in zip(lo, hi)] for lo, hi in zip(cells[:-1], cells[1:])]
    return [[a + b for a, b in zip(lo, hi)] for lo, hi in zip(pairs[:-1], pairs[1:])]


def smooth_second(row):
    pairs = [a + b for a, b in zip(row[:-1], row[1:])]
    return [a + b for a, b in zip([row[0]] + pairs, pairs + [row[-1]])]


def front_kernel(planes, index, left, right, from_left, from_right, w_out, full_out, wg_out, rho_s, both, hot):
    h = lax.axis_index("halo")
    lane = iota((8, NV), 1)
    half_lo = jnp.where(lane == 0, 0.0, 0.5).astype(F32)
    half_hi = jnp.where(lane == NV - 1, 0.0, 0.5).astype(F32)
    on = [jnp.where((h * 4 + q >= 0) & (h * 4 + q < planes[0]), 1.0 / 64, 0.0) for q in range(-3, 7)]

    def place(q):
        if q < 0:
            return from_left, q + 3
        if q < 3:
            return left, q
        if q == 3:
            return right, 2
        return from_right, q - 4

    for q in range(-3, 7):
        ref, p = place(q)
        for c in range(4):
            row = 12 * NV + 4 * p + c
            rho_s[q + 3, c] = jnp.broadcast_to(ref[row : row + 1, :], (8, NV))

    def smooth_third(x):
        return x + half_lo * pltpu.roll(x, 1, 1) + half_hi * pltpu.roll(x, NV - 1, 1)

    def apply(cells, lo):
        dense = [[rho_s[lo + i, c] * x for c, x in enumerate(row)] for i, row in enumerate(cells)]
        plain, dense = smooth_first(cells), smooth_first(dense)
        out = []
        for i, (pr, dr) in enumerate(zip(plain, dense)):
            pr, dr = smooth_second(pr), smooth_second(dr)
            q = lo + 1 + i
            out.append(
                [(rho_s[q, c] * smooth_third(x) + smooth_third(y)) * on[q] for c, (x, y) in enumerate(zip(pr, dr))]
            )
        return out

    def group(g, carry):
        cells = []
        for q in range(-3, 7):
            ref, p = place(q)
            cells.append([ref[pl.ds(pl.multiple_of((4 * p + c) * NV + g * 8, 8), 8), :] for c in range(4)])
        cells = apply(apply(cells, 0), 1)
        rows = pl.ds(pl.multiple_of(g * 8, 8), 8)
        for p in range(4):
            for c in range(4):
                k = 4 * p + c
                both[rows, k * NV : (k + 1) * NV] = cells[p + 1][c]
        cells = apply(cells, 2)
        rows = pl.ds(pl.multiple_of(NV + g * 8, 8), 8)
        for p in range(4):
            for c in range(4):
                k = 4 * p + c
                both[rows, k * NV : (k + 1) * NV] = cells[p][c]
        return carry

    lax.fori_loop(0, NV // 8, group, 0)
    fill_hot(index, hot, F32)
    w = both[:NV, :]
    w_out[...] = w
    gram = dot_nt(w, both[...])
    wg_out[...] = dot_nt(hot[...], w)
    row, col = iota((NV, NV), 0), iota((NV, NV), 1)
    s, c = gram[:, :NV], gram[:, NV:]
    packed = jnp.where(row >= col, s, c)
    diag = jnp.sum(jnp.where(row == col, c, 0.0), axis=0, keepdims=True)
    for peer in range(8):
        full_out[peer, :NV, :] = packed
        full_out[peer, NV:, :] = jnp.broadcast_to(diag, (8, NV))


def fill_hot(index, hot, dtype):
    for part in range(4):
        sub = iota((8, NV), 0)
        col = jnp.zeros((8, NV), jnp.int32)
        for j in range(8):
            col = jnp.where(sub == j, index[0, part // 2, (part % 2) * 8 + j], col)
        lane = iota((8, NV), 1)
        for k in range(16):
            hot[part * 8 : part * 8 + 8, k * NV : (k + 1) * NV] = jnp.where(col == lane + k * NV, 1.0, 0.0).astype(dtype)


def own_kernel(full, wg, stiff, index, li_out, k_out, message, small):
    h = lax.axis_index("halo")
    total = jnp.sum(full[...], axis=0)
    packed, diag = total[:NV, :], total[NV : NV + 1, :]
    row, col = iota((NV, NV), 0), iota((NV, NV), 1)
    mirror = packed.T
    s = jnp.where(row >= col, packed, mirror)
    c = jnp.where(row < col, packed, jnp.where(row > col, mirror, diag))
    (li,) = chol_inv([s])
    k = dot_nt(dot_nn(li, c), li)
    li_out[...] = li
    k_out[...] = k
    rows = dot_nt(wg[...], li)
    small[...] = jnp.zeros((8, NV), F32)
    small[0:2, 0:16] = stiff[0]
    small[2:4, 0:16] = (index[0] + h * NC).astype(F32)
    spread = pltpu.roll(small[...], h * 16, 1)
    mine = k_out[pl.ds(pl.multiple_of(h * 16, 16), 16), :]
    for peer in range(SQ):
        message[peer, :16, :] = mine
        message[peer, 16:48, :] = rows
        message[peer, 48:, :] = spread


def invert(order, inverse):
    for t in range(SQ * SQ):
        inverse[order[t]] = t


def select_kernel(order, got, out, inverse):
    leaf = lax.axis_index("leaf")
    y, z = leaf // SQ, leaf % SQ
    invert(order, inverse)
    for to in range(SQ):
        position = order[to * SQ + z]
        for role in range(1, 4):
            source = inverse[position ^ role]
            part = got[source % SQ]
            out[to, (role - 1) * ROWS : role * ROWS, :] = jnp.where(source // SQ == y, part, 0.0)


def collect_kernel(got, message, out):
    total = jnp.sum(got[...], axis=0)
    own = message[0, 16:, :]
    for peer in range(4):
        out[peer, : 3 * ROWS, :] = total
        out[peer, 3 * ROWS :, :] = own


def solve_kernel(
    order, index, mine, other, k_own, li, w, start, modes_out, reduced_out, inverse, kmat, rmat, big, z_s, hot
):
    h, leaf = lax.axis_index("halo"), lax.axis_index("leaf")
    odd = h % 2
    invert(order, inverse)
    position = order[leaf]
    ids = [leaf] + [inverse[position ^ role] for role in range(1, 4)]
    scale = 0.5 * math.sqrt(NC * 8 / NV)

    def piece(halo, lo, hi):
        a, b = mine[halo // 2, lo:hi, :], other[halo // 2, lo:hi, :]
        return jnp.where(odd == halo % 2, a, b)

    small = []
    kmat[0] = k_own[...]
    for role in range(4):
        base = 3 * ROWS - 16 if role == 0 else (role - 1) * ROWS
        for halo in range(8):
            at = slice(16 * halo, 16 * halo + 16)
            if role:
                kmat[role, at, :] = piece(halo, base, base + 16)
            rmat[0, role, at, :] = piece(halo, base + 16, base + 32)
            rmat[1, role, at, :] = piece(halo, base + 32, base + 48)
        tiles = [piece(halo, base + 48, base + 56) for halo in range(8)]
        small.append(sum(tiles[1:], tiles[0]))

    row, col = iota((NV, NV), 0), iota((NV, NV), 1)
    eye = row == col

    def meet(slot, first, ka, ra, kb, rb, stiff):
        zero = jnp.zeros((NV, NV), F32)
        ra, rb = scale * ra, scale * rb
        r1, r2 = jnp.where(first, ra, rb), jnp.where(first, rb, ra)
        big[slot, :NV, :NV] = jnp.where(first, ka, kb)
        big[slot, :NV, NV : 2 * NV] = zero
        big[slot, :NV, 2 * NV :] = r1.T
        big[slot, NV : 2 * NV, :NV] = zero
        big[slot, NV : 2 * NV, NV : 2 * NV] = jnp.where(first, kb, ka)
        big[slot, NV : 2 * NV, 2 * NV :] = r2.T
        big[slot, 2 * NV :, :NV] = r1
        big[slot, 2 * NV :, NV : 2 * NV] = r2
        big[slot, 2 * NV :, 2 * NV :] = jnp.where(eye, stiff, 0.0)

    def reduce(slots):
        ys = [dot_nn(big[i], dot_nn(big[i], start[...])) for i in slots]
        ps = chol_inv([dot_tn(y, y) for y in ys])
        images = [dot_tn(y, dot_nn(big[i], y)) for i, y in zip(slots, ys)]
        return [dot_nt(y, p) for y, p in zip(ys, ps)], [dot_nt(dot_nn(p, im), p) for p, im in zip(ps, images)]

    firsts = [ids[0] < ids[1], ids[2] < ids[3]]
    for pair in range(2):
        a, b = 2 * pair, 2 * pair + 1
        meet(pair, firsts[pair], kmat[a], rmat[0, a], kmat[b], rmat[0, b], small[a][0:1] + small[b][0:1])
    zs, ks = reduce([0, 1])
    joint = []
    for pair in range(2):
        z = zs[pair]
        lo, hi, zi = z[:NV], z[NV : 2 * NV], z[2 * NV :]
        za, zb = jnp.where(firsts[pair], lo, hi), jnp.where(firsts[pair], hi, lo)
        match = jnp.zeros((NV, NV), F32)
        for role in (2 * pair, 2 * pair + 1):
            up = jnp.sum(jnp.where(eye, small[role][3:4], 0.0), axis=1, keepdims=True)
            match = match + jnp.where(up == small[role][2:3], 1.0, 0.0)
        joint.append(
            dot_nn(rmat[1, 2 * pair], za) + dot_nn(rmat[1, 2 * pair + 1], zb) + math.sqrt(0.5) * dot_nn(match, zi)
        )
        if pair == 0:
            z_s[:NV, :] = za
            z_s[NV:, :] = zi
    first = jnp.minimum(ids[0], ids[1]) < jnp.minimum(ids[2], ids[3])
    stiff = small[0][1:2] + small[1][1:2] + small[2][1:2] + small[3][1:2]
    meet(0, first, ks[0], joint[0], ks[1], joint[1], stiff)
    (z1,), (k1,) = reduce([0])
    reduced_out[...] = k1
    top = jnp.where(first, z1[:NV], z1[NV : 2 * NV])
    at = pl.ds(pl.multiple_of(NV + h * 16, 16), 16)
    low_part = z_s[at, :]
    z_low = z_s[:NV, :]
    z_s[NV:, :] = z1[2 * NV :]
    top_part = z_s[at, :]
    final = math.sqrt(NC * 8)
    mixed = final * dot_tn(top, dot_tn(z_low, li[...]))
    spread = jnp.concatenate([math.sqrt(0.5) * final * dot_nn(low_part, top), 0.5 * final * top_part], axis=0)
    fill_hot(index, hot, F32)
    for k in range(16):
        at = slice(k * NV, (k + 1) * NV)
        part = dot_nn(mixed, w[:, at]) + dot_tn(spread, hot[:, at])
        modes_out[pl.ds(k, NV, stride=16), :] = part


def per_device(start_modes, density, planes, tree_order, iface_index, iface_stiff, reduced_start):
    row_groups = [[y * SQ + z for z in range(SQ)] for y in range(SQ)]
    col_groups = [[y * SQ + z for y in range(SQ)] for z in range(SQ)]
    chips = [[0, 2, 4, 6], [1, 3, 5, 7]]
    edge = 12 * NV + 16
    left, right = pl.pallas_call(
        prep_kernel,
        out_shape=(shape(edge, NV), shape(edge, NV)),
        in_specs=[SM, VM, VM],
        out_specs=(VM, VM),
        scratch_shapes=[pltpu.VMEM((NC, NV), F32)],
        name="prep",
    )(planes, start_modes.reshape(NC, NV), density.reshape(16, NV))
    from_left = lax.ppermute(right, "halo", [(i, i + 1) for i in range(7)])
    from_right = lax.ppermute(left, "halo", [(i + 1, i) for i in range(7)])
    w, full, wg = pl.pallas_call(
        front_kernel,
        out_shape=(shape(NV, NC), shape(8, NV + 8, NV), shape(32, NV)),
        in_specs=[SM, SM, VM, VM, VM, VM],
        out_specs=(VM, VM, VM),
        scratch_shapes=[
            pltpu.VMEM((10, 4, 8, NV), F32),
            pltpu.VMEM((2 * NV, NC), F32),
            pltpu.VMEM((32, NC), F32),
        ],
        name="front",
    )(planes, iface_index, left, right, from_left, from_right)
    full = lax.all_to_all(full, "halo", 0, 0, tiled=True)
    li, k_own, message = pl.pallas_call(
        own_kernel,
        out_shape=(shape(NV, NV), shape(NV, NV), shape(SQ, ROWS, NV)),
        in_specs=[VM, VM, VM, VM],
        out_specs=(VM, VM, VM),
        scratch_shapes=[pltpu.VMEM((8, NV), F32)],
        name="own",
    )(full, wg, iface_stiff, iface_index)
    along = lax.all_to_all(message, "leaf", 0, 0, tiled=True, axis_index_groups=row_groups)
    chosen = pl.pallas_call(
        select_kernel,
        out_shape=shape(SQ, 3 * ROWS, NV),
        in_specs=[SM, VM],
        out_specs=VM,
        scratch_shapes=[pltpu.SMEM((SQ * SQ,), jnp.int32)],
        name="select",
    )(tree_order, along)
    across = lax.all_to_all(chosen, "leaf", 0, 0, tiled=True, axis_index_groups=col_groups)
    gathered = pl.pallas_call(
        collect_kernel,
        out_shape=shape(4, AG, NV),
        in_specs=[VM, VM],
        out_specs=VM,
        name="collect",
    )(across, message)
    mine = lax.all_to_all(gathered, "halo", 0, 0, tiled=True, axis_index_groups=chips)
    other = lax.ppermute(mine, "halo", [(i, i ^ 1) for i in range(8)])
    modes, reduced = pl.pallas_call(
        solve_kernel,
        out_shape=(shape(NC, NV), shape(NV, NV)),
        in_specs=[SM, SM, VM, VM, VM, VM, VM, VM],
        out_specs=(VM, VM),
        scratch_shapes=[
            pltpu.SMEM((SQ * SQ,), jnp.int32),
            pltpu.VMEM((4, NV, NV), F32),
            pltpu.VMEM((2, 4, NV, NV), F32),
            pltpu.VMEM((2, 3 * NV, 3 * NV), F32),
            pltpu.VMEM((2 * NV, NV), F32),
            pltpu.VMEM((32, NC), F32),
        ],
        name="solve",
    )(tree_order, iface_index, mine, other, k_own, li, w, reduced_start)
    return modes.reshape(1, NV, 4, 4, NV), reduced[None]


def solution(mesh):
    return jax.shard_map(
        per_device,
        mesh=mesh,
        in_specs=(
            P("leaf", None, "halo", None, None),
            P("leaf", "halo", None, None),
            P("leaf"),
            P(),
            P("leaf", None, "halo"),
            P("leaf", None, "halo"),
            P(),
        ),
        out_specs=(P("leaf", None, "halo", None, None), P("leaf", None, None)),
        check_vma=False,
    )
```

time: 410 us -> 146 us (0.36); the launches traced: 403 us -> 145 us
  other arithmetic: 140 us -> 0 us
  starting transfers between devices: 124 us -> 17.7 us
  waiting for transfers between devices: 90.9 us -> 10.5 us
  blocking collectives: 0 us -> 66.5 us
  Pallas kernels: 0 us -> 47.5 us
  matrix products: 22 us -> 0 us
  local copies, waits for them, and re-layouts: 17.4 us -> 1.66 us
  between operations: 8.45 us -> 1.31 us
    another operation x32 -> x0, other arithmetic: 116 us -> none  [the longest x12 49.9 us: reduce_solve(): lower_factor = jnp.linalg.cholesky(gram_small)]
    all_to_all x13 -> x0, starting transfers between devices: 95.4 us -> none  [sent_to_all(): lax.all_to_all(jnp.broadcast_to(array[None], (size, *array.shape)), axis,...]
    all_to_all x13 -> x0, waiting for transfers between devices: 87.3 us -> none  [sent_to_all(): lax.all_to_all(jnp.broadcast_to(array[None], (size, *array.shape)), axis,...]
    all_to_all x0 -> x4, blocking collectives: none -> 66.5 us  [the longest x1 25 us: per_device(): lax.all_to_all(chosen, 'leaf', 0, 0, tiled=True, axis_index_groups=col_gr...]
    pallas_call x0 -> x6, Pallas kernels: none -> 47.5 us  [the longest x1 21.8 us: per_device(): pl.pallas_call(solve_kernel, out_shape=(shape(NC, NV), shape(NV, NV)), in...]
    dot_general x26 -> x0, matrix products: 18.9 us -> none  [the longest x2 3.03 us: gram_local(): return jnp.einsum('kp,jp->kj', left_rows, right_rows, precision=EXACT)]
    add x9 -> x0, other arithmetic: 14.1 us -> none  [the longest x6 10.3 us: axis_smooth(): 0.5 * lax.slice_in_dim(padded, 0, extent, axis=axis_number)]
    ppermute x8 -> x3, starting transfers between devices: 28.8 us -> 17.7 us  [the longest x1 8.73 us: per_device(): from_right = lax.ppermute(left, 'halo', [(i + 1, i) for i in range(7)])]
  transfers between devices with their start and end apart: 21 -> 3, of which waited for: 14 -> 3; matrix products, arithmetic and copies ran while one was open for 28% -> 0% of each run, Pallas kernels for 0% -> 0%
where the time goes in v1:
time: 146 us; the launch traced here: 145 us
  blocking collectives  66.5 us (46%)
  Pallas kernels  47.5 us (33%)
  starting transfers between devices  17.7 us (12%)
  waiting for transfers between devices  10.5 us (7%)
  local copies, waits for them, and re-layouts  1.66 us (1%)
    all_to_all x1, blocking collectives, per_device(): lax.all_to_all(chosen, 'leaf', 0, 0, tiled=True, axis_index_groups=col_gr...  25 us
    pallas_call x1, Pallas kernels, per_device(): pl.pallas_call(solve_kernel, out_shape=(shape(NC, NV), shape(NV, NV)), in...  21.8 us
    all_to_all x1, blocking collectives, per_device(): lax.all_to_all(message, 'leaf', 0, 0, tiled=True, axis_index_groups=row_g...  17.3 us
    all_to_all x1, blocking collectives, per_device(): full = lax.all_to_all(full, 'halo', 0, 0, tiled=True)  14.3 us
    pallas_call x1, Pallas kernels, per_device(): pl.pallas_call(front_kernel, out_shape=(shape(NV, NC), shape(8, NV + 8, N...  12.6 us
    all_to_all x1, blocking collectives, per_device(): lax.all_to_all(gathered, 'halo', 0, 0, tiled=True, axis_index_groups=chips)  9.84 us
    ppermute x1, starting transfers between devices, per_device(): from_right = lax.ppermute(left, 'halo', [(i + 1, i) for i in range(7)])  8.73 us
    ppermute x1, starting transfers between devices, per_device(): other = lax.ppermute(mine, 'halo', [(i, i ^ 1) for i in range(8)])  7.07 us
  transfers between devices with their start and end apart: 3, of which 3 were waited for; matrix products, arithmetic and copies ran while one was open for 0% of the time, Pallas kernels for 0%

profile of v1, /device:TPU:1, one launch (start us, length us, event | category | flops | bytes accessed | tf_op | source)
XLA Modules:
  0.0 145.2 jit_solution(11750271696587936207)
XLA Ops:
  1.3 2.6 %prep.1 = (f32[1552,128]{1,0:T(8,128)}, f32[1552,128]{1,0:T(8,128)}) custom-call(s32[1]{0:T(128)S(6)} %copy.9.planes, bf16[2048,128]{1,0:T(8,128)(2,1)} %bitcast.4, f32[16,128]{1,0:T(8,128)} %bitcast.5), custom_call_target="tpu_custom_call" | custom-call | tf_op jit(solution)/shard_map/prep/pallas_call | solution.py:340
  3.9 8.7 %collective-permute-start.1 = (f32[1552,128]{1,0:T(8,128)}, f32[1552,128]{1,0:T(8,128)S(1)}, u32[]{:S(2)}, u32[]{:S(2)}) collective-permute-start(f32[1552,128]{1,0:T(8,128)} %get-tuple-element.12.left), channel_id=1, source_target_pairs={{64,0},{128,64},{192,128},{256,192},{320,256},{384,320},{448,384},... | collective-permute-start | bytes 2383880 | tf_op jit(solution)/shard_map/ppermute | solution.py:349
  12.6 1.9 %collective-permute-start = (f32[1552,128]{1,0:T(8,128)}, f32[1552,128]{1,0:T(8,128)S(1)}, u32[]{:S(2)}, u32[]{:S(2)}) collective-permute-start(f32[1552,128]{1,0:T(8,128)} %get-tuple-element.13.right), channel_id=1, source_target_pairs={{0,64},{64,128},{128,192},{192,256},{256,320},{320,384},{384,448},... | collective-permute-start | bytes 2383880 | tf_op jit(solution)/shard_map/ppermute | solution.py:348
  14.6 3.8 %collective-permute-done.1.from_right = f32[1552,128]{1,0:T(8,128)S(1)} collective-permute-done((f32[1552,128]{1,0:T(8,128)}, f32[1552,128]{1,0:T(8,128)S(1)}, u32[]{:S(2)}, u32[]{:S(2)}) %collective-permute-start.1) | collective-permute-done | bytes 794656 | tf_op jit(solution)/shard_map/ppermute | solution.py:349
  18.3 0.0 copy-start.1
  18.4 5.5 %collective-permute-done.from_left = f32[1552,128]{1,0:T(8,128)S(1)} collective-permute-done((f32[1552,128]{1,0:T(8,128)}, f32[1552,128]{1,0:T(8,128)S(1)}, u32[]{:S(2)}, u32[]{:S(2)}) %collective-permute-start) | collective-permute-done | bytes 794656 | tf_op jit(solution)/shard_map/ppermute | solution.py:348
  23.9 0.0 copy-done.1
  23.9 0.0 copy-start.2
  23.9 0.9 copy-done.2
  24.8 12.6 %front.1 = (f32[128,2048]{1,0:T(8,128)}, f32[8,136,128]{2,1,0:T(8,128)}, f32[32,128]{1,0:T(8,128)}) custom-call(s32[1]{0:T(128)S(6)} %copy.9.planes, s32[1,2,16]{2,1,0:T(2,128)} %index.5, f32[1552,128]{1,0:T(8,128)} %get-tuple-element.12.left, f32[1552,128]{1,0:T(8,128)} %get-tuple-element.13.right, f32[1552,128]{1,0:T(8,128)} %copy-done.2, ...), custom_call_target="tpu_custom_call" | custom-call | tf_op jit(solution)/shard_map/front/pallas_call | solution.py:350
  37.4 14.3 %all_to_all.20.full = f32[8,136,128]{2,1,0:T(8,128)} all-to-all(f32[8,136,128]{2,1,0:T(8,128)} %get-tuple-element.14), channel_id=1, replica_groups=mesh['halo'=8,'leaf'=64] {'halo'}, dimensions={0} | all-to-all | bytes 1114112 | tf_op jit(solution)/shard_map/all_to_all | solution.py:362
  51.7 6.5 %own.1 = (f32[128,128]{1,0:T(8,128)}, f32[128,128]{1,0:T(8,128)}, f32[8,56,128]{2,1,0:T(8,128)}) custom-call(f32[8,136,128]{2,1,0:T(8,128)} %all_to_all.20.full, f32[32,128]{1,0:T(8,128)} %get-tuple-element.15.wg, f32[1,2,16]{2,1,0:T(2,128)} %stiff.1, s32[1,2,16]{2,1,0:T(2,128)} %index.5), custom_call_target="tpu_custom_call" | custom-call | tf_op jit(solution)/shard_map/own/pallas_call | solution.py:363
  58.2 17.3 %all_to_all.21.got = f32[8,56,128]{2,1,0:T(8,128)} all-to-all(f32[8,56,128]{2,1,0:T(8,128)} %get-tuple-element.16.message), channel_id=1, replica_groups={{0,1,2,3,4,5,6,7},{8,9,10,11,12,13,14,15},{16,17,18,19,20,21,22,23},{24..., dimensions={0} | all-to-all | bytes 458752 | tf_op jit(solution)/shard_map/all_to_all | solution.py:371
  75.5 2.0 %select.1 = f32[8,168,128]{2,1,0:T(8,128)} custom-call(s32[64]{0:T(128)} %order.3, f32[8,56,128]{2,1,0:T(8,128)} %all_to_all.21.got), custom_call_target="tpu_custom_call" | custom-call | tf_op jit(solution)/shard_map/select/pallas_call | solution.py:372
  77.5 25.0 %all_to_all.22.got = f32[8,168,128]{2,1,0:T(8,128)} all-to-all(f32[8,168,128]{2,1,0:T(8,128)} %select.1), channel_id=1, replica_groups={{0,8,16,24,32,40,48,56},{1,9,17,25,33,41,49,57},{2,10,18,26,34,42,50,58..., dimensions={0} | all-to-all | bytes 1376256 | tf_op jit(solution)/shard_map/all_to_all | solution.py:380
  102.6 1.9 %collect.1 = f32[4,208,128]{2,1,0:T(8,128)} custom-call(f32[8,168,128]{2,1,0:T(8,128)} %all_to_all.22.got, f32[8,56,128]{2,1,0:T(8,128)} %get-tuple-element.16.message), custom_call_target="tpu_custom_call" | custom-call | tf_op jit(solution)/shard_map/collect/pallas_call | solution.py:381
  104.5 9.8 %all_to_all.23.mine = f32[4,208,128]{2,1,0:T(8,128)S(1)} all-to-all(f32[4,208,128]{2,1,0:T(8,128)} %collect.1), channel_id=1, replica_groups={{0,128,256,384},{64,192,320,448},{1,129,257,385},{65,193,321,449},{2,13..., dimensions={0} | all-to-all | bytes 851968 | tf_op jit(solution)/shard_map/all_to_all | solution.py:388
  114.3 0.0 copy-start
  114.3 7.1 %collective-permute-start.2 = (f32[4,208,128]{2,1,0:T(8,128)S(1)}, f32[4,208,128]{2,1,0:T(8,128)S(1)}, u32[]{:S(2)}, u32[]{:S(2)}) collective-permute-start(f32[4,208,128]{2,1,0:T(8,128)S(1)} %all_to_all.23.mine), channel_id=1, source_target_pairs={{0,64},{64,0},{128,192},{192,128},{256,320},{320,256},{384,448},{4... | collective-permute-start | bytes 1277960 | tf_op jit(solution)/shard_map/ppermute | solution.py:389
  121.4 1.2 collective-permute-done.2.other
  122.6 0.0 copy-start.3
  122.6 0.0 copy-done
  122.6 0.8 copy-done.3
  123.4 21.8 %solve.1 = (f32[2048,128]{1,0:T(8,128)}, f32[128,128]{1,0:T(8,128)}) custom-call(s32[64]{0:T(128)} %order.3, s32[1,2,16]{2,1,0:T(2,128)} %index.5, f32[4,208,128]{2,1,0:T(8,128)} %copy-done, f32[4,208,128]{2,1,0:T(8,128)} %copy-done.3, f32[128,128]{1,0:T(8,128)} %get-tuple-element.17.k_own, f32[128,128]{1,0:T(8,128)} %get-tuple-element.18.li, ...), custom_call_target="tpu_custom_call" | custom-call | tf_op jit(solution)/shard_map/solve/pallas_call | solution.py:390
Async XLA Ops:
  3.9 14.5 %collective-permute-start.1 = (f32[1552,128]{1,0:T(8,128)}, f32[1552,128]{1,0:T(8,128)S(1)}, u32[]{:S(2)}, u32[]{:S(2)}) collective-permute-start(f32[1552,128]{1,0:T(8,128)} %get-tuple-element.12.left), channel_id=1, source_target_pairs={{64,0},{128,64},{192,128},{256,192},{320,256},{384,320},{448,384},... | collective-permute-start | bytes 2383880 | tf_op jit(solution)/shard_map/ppermute | solution.py:349
  12.6 11.2 %collective-permute-start = (f32[1552,128]{1,0:T(8,128)}, f32[1552,128]{1,0:T(8,128)S(1)}, u32[]{:S(2)}, u32[]{:S(2)}) collective-permute-start(f32[1552,128]{1,0:T(8,128)} %get-tuple-element.13.right), channel_id=1, source_target_pairs={{0,64},{64,128},{128,192},{192,256},{256,320},{320,384},{384,448},... | collective-permute-start | bytes 2383880 | tf_op jit(solution)/shard_map/ppermute | solution.py:348
  18.3 5.5 %copy-start.1 = (f32[1552,128]{1,0:T(8,128)}, f32[1552,128]{1,0:T(8,128)S(1)}, u32[]{:S(2)}) copy-start(f32[1552,128]{1,0:T(8,128)S(1)} %collective-permute-done.1.from_right) | copy-start | bytes 2383876
  23.9 0.9 copy-start.2
  114.3 8.3 %copy-start = (f32[4,208,128]{2,1,0:T(8,128)}, f32[4,208,128]{2,1,0:T(8,128)S(1)}, u32[]{:S(2)}) copy-start(f32[4,208,128]{2,1,0:T(8,128)S(1)} %all_to_all.23.mine) | copy-start | bytes 1277956
  114.3 8.3 %collective-permute-start.2 = (f32[4,208,128]{2,1,0:T(8,128)S(1)}, f32[4,208,128]{2,1,0:T(8,128)S(1)}, u32[]{:S(2)}, u32[]{:S(2)}) collective-permute-start(f32[4,208,128]{2,1,0:T(8,128)S(1)} %all_to_all.23.mine), channel_id=1, source_target_pairs={{0,64},{64,0},{128,192},{192,128},{256,320},{320,256},{384,448},{4... | collective-permute-start | bytes 1277960 | tf_op jit(solution)/shard_map/ppermute | solution.py:389
  122.6 0.8 copy-start.3

commit v2 on v1

--- a/solution.py
+++ b/solution.py
@@ -12,7 +12,7 @@
 NV = 128
 NC = 2048
 SQ = 8
-ROWS = 56
+ROWS = 48
 AG = 3 * ROWS + 40
 VM = pl.BlockSpec(memory_space=pltpu.VMEM)
 SM = pl.BlockSpec(memory_space=pltpu.SMEM)
@@ -32,6 +32,10 @@
 
 def iota(shape, dim):
     return lax.broadcasted_iota(jnp.int32, shape, dim)
+
+
+def grant(mib):
+    return pltpu.CompilerParams(vmem_limit_bytes=mib << 20)
 
 
 def shape(*dims):
@@ -208,12 +212,17 @@
     small[...] = jnp.zeros((8, NV), F32)
     small[0:2, 0:16] = stiff[0]
     small[2:4, 0:16] = (index[0] + h * NC).astype(F32)
-    spread = pltpu.roll(small[...], h * 16, 1)
-    mine = k_out[pl.ds(pl.multiple_of(h * 16, 16), 16), :]
+    lane, sub = iota((8, NV), 1), iota((8, NV), 0)
+    tile = small[...]
+    tile = jnp.where(sub < 4, tile, pltpu.roll(pltpu.roll(tile, NV - 8, 1), 4, 0))
+    tile = pltpu.roll(tile, h * 16, 1)
+    upper = k_out[pl.ds(pl.multiple_of(h * 16, 16), 8), :]
+    lower = k_out[pl.ds(pl.multiple_of(h * 16 + 8, 8), 8), :]
+    lower = jnp.where((lane >= h * 16) & (lane < h * 16 + 8), tile, lower)
     for peer in range(SQ):
-        message[peer, :16, :] = mine
-        message[peer, 16:48, :] = rows
-        message[peer, 48:, :] = spread
+        message[peer, :8, :] = upper
+        message[peer, 8:16, :] = lower
+        message[peer, 16:, :] = rows
 
 
 def invert(order, inverse):
@@ -229,15 +238,20 @@
         position = order[to * SQ + z]
         for role in range(1, 4):
             source = inverse[position ^ role]
-            part = got[source % SQ]
-            out[to, (role - 1) * ROWS : role * ROWS, :] = jnp.where(source // SQ == y, part, 0.0)
-
-
-def collect_kernel(got, message, out):
-    total = jnp.sum(got[...], axis=0)
-    own = message[0, 16:, :]
+            @pl.when(source // SQ == y)
+            def _(to=to, role=role, source=source):
+                out[to, (role - 1) * ROWS : role * ROWS, :] = got[source % SQ]
+
+
+def collect_kernel(order, got, message, out, inverse):
+    leaf = lax.axis_index("leaf")
+    invert(order, inverse)
+    position = order[leaf]
+    parts = [got[inverse[position ^ r] // SQ, (r - 1) * ROWS : r * ROWS, :] for r in range(1, 4)]
+    own = message[0, 8:, :]
     for peer in range(4):
-        out[peer, : 3 * ROWS, :] = total
+        for r in range(3):
+            out[peer, r * ROWS : (r + 1) * ROWS, :] = parts[r]
         out[peer, 3 * ROWS :, :] = own
 
 
@@ -255,21 +269,27 @@
         a, b = mine[halo // 2, lo:hi, :], other[halo // 2, lo:hi, :]
         return jnp.where(odd == halo % 2, a, b)
 
+    row, col = iota((NV, NV), 0), iota((NV, NV), 1)
+    eye = row == col
+    lane = iota((8, NV), 1)
     small = []
     kmat[0] = k_own[...]
     for role in range(4):
-        base = 3 * ROWS - 16 if role == 0 else (role - 1) * ROWS
+        base = 3 * ROWS - 8 if role == 0 else (role - 1) * ROWS
+        tile = jnp.zeros((8, NV), F32)
         for halo in range(8):
             at = slice(16 * halo, 16 * halo + 16)
+            lower = piece(halo, base + 8, base + 16)
             if role:
-                kmat[role, at, :] = piece(halo, base, base + 16)
+                kmat[role, 16 * halo : 16 * halo + 8, :] = piece(halo, base, base + 8)
+                kmat[role, 16 * halo + 8 : 16 * halo + 16, :] = lower
             rmat[0, role, at, :] = piece(halo, base + 16, base + 32)
             rmat[1, role, at, :] = piece(halo, base + 32, base + 48)
-        tiles = [piece(halo, base + 48, base + 56) for halo in range(8)]
-        small.append(sum(tiles[1:], tiles[0]))
-
-    row, col = iota((NV, NV), 0), iota((NV, NV), 1)
-    eye = row == col
+            tile = jnp.where((lane >= 16 * halo) & (lane < 16 * halo + 8), lower, tile)
+        small.append(tile + pltpu.roll(pltpu.roll(tile, 8, 1), 4, 0))
+        if role:
+            raw = kmat[role]
+            kmat[role] = jnp.where(row <= col, raw, raw.T)
 
     def meet(slot, first, ka, ra, kb, rb, stiff):
         zero = jnp.zeros((NV, NV), F32)
@@ -344,6 +364,7 @@
         out_specs=(VM, VM),
         scratch_shapes=[pltpu.VMEM((NC, NV), F32)],
         name="prep",
+        compiler_params=grant(8),
     )(planes, start_modes.reshape(NC, NV), density.reshape(16, NV))
     from_left = lax.ppermute(right, "halo", [(i, i + 1) for i in range(7)])
     from_right = lax.ppermute(left, "halo", [(i + 1, i) for i in range(7)])
@@ -358,6 +379,7 @@
             pltpu.VMEM((32, NC), F32),
         ],
         name="front",
+        compiler_params=grant(24),
     )(planes, iface_index, left, right, from_left, from_right)
     full = lax.all_to_all(full, "halo", 0, 0, tiled=True)
     li, k_own, message = pl.pallas_call(
@@ -367,6 +389,7 @@
         out_specs=(VM, VM, VM),
         scratch_shapes=[pltpu.VMEM((8, NV), F32)],
         name="own",
+        compiler_params=grant(8),
     )(full, wg, iface_stiff, iface_index)
     along = lax.all_to_all(message, "leaf", 0, 0, tiled=True, axis_index_groups=row_groups)
     chosen = pl.pallas_call(
@@ -376,15 +399,18 @@
         out_specs=VM,
         scratch_shapes=[pltpu.SMEM((SQ * SQ,), jnp.int32)],
         name="select",
+        compiler_params=grant(4),
     )(tree_order, along)
     across = lax.all_to_all(chosen, "leaf", 0, 0, tiled=True, axis_index_groups=col_groups)
     gathered = pl.pallas_call(
         collect_kernel,
         out_shape=shape(4, AG, NV),
-        in_specs=[VM, VM],
+        in_specs=[SM, VM, VM],
         out_specs=VM,
+        scratch_shapes=[pltpu.SMEM((SQ * SQ,), jnp.int32)],
         name="collect",
-    )(across, message)
+        compiler_params=grant(4),
+    )(tree_order, across, message)
     mine = lax.all_to_all(gathered, "halo", 0, 0, tiled=True, axis_index_groups=chips)
     other = lax.ppermute(mine, "halo", [(i, i ^ 1) for i in range(8)])
     modes, reduced = pl.pallas_call(
@@ -401,6 +427,7 @@
             pltpu.VMEM((32, NC), F32),
         ],
         name="solve",
+        compiler_params=grant(20),
     )(tree_order, iface_index, mine, other, k_own, li, w, reduced_start)
     return modes.reshape(1, NV, 4, 4, NV), reduced[None]
 

time: 146 us -> 132 us (0.904)
  Pallas kernels: 47.5 us -> 38.2 us
  blocking collectives: 66.5 us -> 61.3 us
    all_to_all x1, blocking collectives: 25 us -> 22.4 us  [per_device(): lax.all_to_all(chosen, 'leaf', 0, 0, tiled=True, axis_index_groups=col_gr...]
    pallas_call x1, Pallas kernels: 12.6 us -> 10.4 us  [per_device(): pl.pallas_call(front_kernel, out_shape=(shape(NV, NC), shape(8, NV + 8, N...]
    pallas_call x1, Pallas kernels: 2.62 us -> 0.53 us  [per_device(): pl.pallas_call(prep_kernel, out_shape=(shape(edge, NV), shape(edge, NV)),...]
    pallas_call x1, Pallas kernels: 6.51 us -> 4.71 us  [per_device(): pl.pallas_call(own_kernel, out_shape=(shape(NV, NV), shape(NV, NV), shape...]
where the time goes in v2:
time: 132 us; the launch traced here: 131 us
  blocking collectives  61.3 us (46%)
  Pallas kernels  38.2 us (29%)
  starting transfers between devices  18 us (14%)
  waiting for transfers between devices  10.1 us (8%)
  local copies, waits for them, and re-layouts  2.43 us (2%)
  between operations  1.37 us (1%)
    all_to_all x1, blocking collectives, per_device(): lax.all_to_all(chosen, 'leaf', 0, 0, tiled=True, axis_index_groups=col_gr...  22.4 us
    pallas_call x1, Pallas kernels, per_device(): pl.pallas_call(solve_kernel, out_shape=(shape(NC, NV), shape(NV, NV)), in...  20.9 us
    all_to_all x1, blocking collectives, per_device(): lax.all_to_all(message, 'leaf', 0, 0, tiled=True, axis_index_groups=row_g...  16.2 us
    all_to_all x1, blocking collectives, per_device(): full = lax.all_to_all(full, 'halo', 0, 0, tiled=True)  14.1 us
    pallas_call x1, Pallas kernels, per_device(): pl.pallas_call(front_kernel, out_shape=(shape(NV, NC), shape(8, NV + 8, N...  10.4 us
    ppermute x1, starting transfers between devices, per_device(): from_right = lax.ppermute(left, 'halo', [(i + 1, i) for i in range(7)])  8.75 us
    all_to_all x1, blocking collectives, per_device(): lax.all_to_all(gathered, 'halo', 0, 0, tiled=True, axis_index_groups=chips)  8.66 us
    ppermute x1, starting transfers between devices, per_device(): other = lax.ppermute(mine, 'halo', [(i, i ^ 1) for i in range(8)])  7.31 us
  transfers between devices with their start and end apart: 3, of which 3 were waited for; matrix products, arithmetic and copies ran while one was open for 0% of the time, Pallas kernels for 0%

profile of v2, /device:TPU:1, one launch (start us, length us, event | category | flops | bytes accessed | tf_op | source)
XLA Modules:
  0.0 131.5 jit_solution(5820229934884411650)
XLA Ops:
  1.3 0.0 copy-start
  1.3 1.0 copy-done
  2.3 0.0 copy-start.3
  2.3 0.7 copy-done.3
  3.0 0.5 prep.1
  3.5 0.0 copy-start.2
  3.6 8.7 %collective-permute-start.1 = (f32[1552,128]{1,0:T(8,128)S(1)}, f32[1552,128]{1,0:T(8,128)S(1)}, u32[]{:S(2)}, u32[]{:S(2)}) collective-permute-start(f32[1552,128]{1,0:T(8,128)S(1)} %get-tuple-element.12.left), channel_id=1, source_target_pairs={{64,0},{128,64},{192,128},{256,192},{320,256},{384,320},{448,384},... | collective-permute-start | bytes 2383880 | tf_op jit(solution)/shard_map/ppermute | solution.py:370
  12.3 1.9 %collective-permute-start = (f32[1552,128]{1,0:T(8,128)S(1)}, f32[1552,128]{1,0:T(8,128)S(1)}, u32[]{:S(2)}, u32[]{:S(2)}) collective-permute-start(f32[1552,128]{1,0:T(8,128)S(1)} %get-tuple-element.13.right), channel_id=1, source_target_pairs={{0,64},{64,128},{128,192},{192,256},{256,320},{320,384},{384,448},... | collective-permute-start | bytes 2383880 | tf_op jit(solution)/shard_map/ppermute | solution.py:369
  14.2 3.6 %collective-permute-done.1.from_right = f32[1552,128]{1,0:T(8,128)S(1)} collective-permute-done((f32[1552,128]{1,0:T(8,128)S(1)}, f32[1552,128]{1,0:T(8,128)S(1)}, u32[]{:S(2)}, u32[]{:S(2)}) %collective-permute-start.1) | collective-permute-done | bytes 794656 | tf_op jit(solution)/shard_map/ppermute | solution.py:370
  17.8 5.4 %collective-permute-done.from_left = f32[1552,128]{1,0:T(8,128)S(1)} collective-permute-done((f32[1552,128]{1,0:T(8,128)S(1)}, f32[1552,128]{1,0:T(8,128)S(1)}, u32[]{:S(2)}, u32[]{:S(2)}) %collective-permute-start) | collective-permute-done | bytes 794656 | tf_op jit(solution)/shard_map/ppermute | solution.py:369
  23.2 0.0 copy-done.2
  23.2 10.4 %front.1 = (f32[128,2048]{1,0:T(8,128)S(1)}, f32[8,136,128]{2,1,0:T(8,128)S(1)}, f32[32,128]{1,0:T(8,128)S(1)}) custom-call(s32[1]{0:T(128)S(6)} %copy.9.planes, s32[1,2,16]{2,1,0:T(2,128)S(1)} %copy-done.2, f32[1552,128]{1,0:T(8,128)S(1)} %get-tuple-element.12.left, f32[1552,128]{1,0:T(8,128)S(1)} %get-tuple-element.13.right, ...), custom_call_target="tpu_custom_call" | custom-call | tf_op jit(solution)/shard_map/front/pallas_call | solution.py:371
  33.7 14.1 %all_to_all.20.full = f32[8,136,128]{2,1,0:T(8,128)S(1)} all-to-all(f32[8,136,128]{2,1,0:T(8,128)S(1)} %get-tuple-element.14), channel_id=1, replica_groups=mesh['halo'=8,'leaf'=64] {'halo'}, dimensions={0} | all-to-all | bytes 1114112 | tf_op jit(solution)/shard_map/all_to_all | solution.py:384
  47.8 0.0 copy-start.5
  47.8 0.7 copy-done.5
  48.4 4.7 %own.1 = (f32[128,128]{1,0:T(8,128)S(1)}, f32[128,128]{1,0:T(8,128)S(1)}, f32[8,48,128]{2,1,0:T(8,128)S(1)}) custom-call(f32[8,136,128]{2,1,0:T(8,128)S(1)} %all_to_all.20.full, f32[32,128]{1,0:T(8,128)S(1)} %get-tuple-element.15.wg, f32[1,2,16]{2,1,0:T(2,128)S(1)} %copy-done.5, s32[1,2,16]{2,1,0:T(2,128)S(1)} %copy-done.2), custom_call_target="tpu_custom_call" | custom-call | tf_op jit(solution)/shard_map/own/pallas_call | solution.py:385
  53.2 0.0 copy-start.4
  53.2 16.2 %all_to_all.21.got = f32[8,48,128]{2,1,0:T(8,128)S(1)} all-to-all(f32[8,48,128]{2,1,0:T(8,128)S(1)} %get-tuple-element.16.message), channel_id=1, replica_groups={{0,1,2,3,4,5,6,7},{8,9,10,11,12,13,14,15},{16,17,18,19,20,21,22,23},{24..., dimensions={0} | all-to-all | bytes 393216 | tf_op jit(solution)/shard_map/all_to_all | solution.py:394
  69.4 0.0 copy-done.4
  69.4 1.0 select.1
  70.4 22.4 %all_to_all.22.got = f32[8,144,128]{2,1,0:T(8,128)S(1)} all-to-all(f32[8,144,128]{2,1,0:T(8,128)S(1)} %select.1), channel_id=1, replica_groups={{0,8,16,24,32,40,48,56},{1,9,17,25,33,41,49,57},{2,10,18,26,34,42,50,58..., dimensions={0} | all-to-all | bytes 1179648 | tf_op jit(solution)/shard_map/all_to_all | solution.py:404
  92.8 0.6 collect.1
  93.4 0.0 copy-start.1
  93.4 8.7 %all_to_all.23.mine = f32[4,184,128]{2,1,0:T(8,128)S(1)} all-to-all(f32[4,184,128]{2,1,0:T(8,128)S(1)} %collect.1), channel_id=1, replica_groups={{0,128,256,384},{64,192,320,448},{1,129,257,385},{65,193,321,449},{2,13..., dimensions={0} | all-to-all | bytes 753664 | tf_op jit(solution)/shard_map/all_to_all | solution.py:414
  102.1 7.3 %collective-permute-start.2 = (f32[4,184,128]{2,1,0:T(8,128)S(1)}, f32[4,184,128]{2,1,0:T(8,128)S(1)}, u32[]{:S(2)}, u32[]{:S(2)}) collective-permute-start(f32[4,184,128]{2,1,0:T(8,128)S(1)} %all_to_all.23.mine), channel_id=1, source_target_pairs={{0,64},{64,0},{128,192},{192,128},{256,320},{320,256},{384,448},{4... | collective-permute-start | bytes 1130504 | tf_op jit(solution)/shard_map/ppermute | solution.py:415
  109.4 1.1 collective-permute-done.2.other
  110.6 0.0 copy-done.1
  110.6 20.9 %solve.1 = (f32[2048,128]{1,0:T(8,128)}, f32[128,128]{1,0:T(8,128)}) custom-call(s32[64]{0:T(128)S(1)} %copy-done.4, s32[1,2,16]{2,1,0:T(2,128)S(1)} %copy-done.2, f32[4,184,128]{2,1,0:T(8,128)S(1)} %all_to_all.23.mine, f32[4,184,128]{2,1,0:T(8,128)S(1)} %collective-permute-done.2.other, f32[128,128]{1,0:T(8,128)S(1)} %get-tuple-element.17.k_own, ...), custom_call_target="tpu_custom_call" | custom-call | tf_op jit(solution)/shard_map/solve/pallas_call | solution.py:416
Async XLA Ops:
  1.3 1.0 copy-start
  2.3 0.7 copy-start.3
  3.5 19.7 %copy-start.2 = (s32[1,2,16]{2,1,0:T(2,128)S(1)}, s32[1,2,16]{2,1,0:T(2,128)}, u32[]{:S(2)}) copy-start(s32[1,2,16]{2,1,0:T(2,128)} %index.5) | copy-start | bytes 388
  3.6 14.3 %collective-permute-start.1 = (f32[1552,128]{1,0:T(8,128)S(1)}, f32[1552,128]{1,0:T(8,128)S(1)}, u32[]{:S(2)}, u32[]{:S(2)}) collective-permute-start(f32[1552,128]{1,0:T(8,128)S(1)} %get-tuple-element.12.left), channel_id=1, source_target_pairs={{64,0},{128,64},{192,128},{256,192},{320,256},{384,320},{448,384},... | collective-permute-start | bytes 2383880 | tf_op jit(solution)/shard_map/ppermute | solution.py:370
  12.3 10.9 %collective-permute-start = (f32[1552,128]{1,0:T(8,128)S(1)}, f32[1552,128]{1,0:T(8,128)S(1)}, u32[]{:S(2)}, u32[]{:S(2)}) collective-permute-start(f32[1552,128]{1,0:T(8,128)S(1)} %get-tuple-element.13.right), channel_id=1, source_target_pairs={{0,64},{64,128},{128,192},{192,256},{256,320},{320,384},{384,448},... | collective-permute-start | bytes 2383880 | tf_op jit(solution)/shard_map/ppermute | solution.py:369
  47.8 0.7 copy-start.5
  53.2 16.2 %copy-start.4 = (s32[64]{0:T(128)S(1)}, s32[64]{0:T(128)}, u32[]{:S(2)}) copy-start(s32[64]{0:T(128)} %order.5) | copy-start | bytes 772
  93.4 17.1 %copy-start.1 = (f32[384,128]{1,0:T(8,128)S(1)}, f32[384,128]{1,0:T(8,128)}, u32[]{:S(2)}) copy-start(f32[384,128]{1,0:T(8,128)} %start.1) | copy-start | bytes 589828
  102.1 8.4 %collective-permute-start.2 = (f32[4,184,128]{2,1,0:T(8,128)S(1)}, f32[4,184,128]{2,1,0:T(8,128)S(1)}, u32[]{:S(2)}, u32[]{:S(2)}) collective-permute-start(f32[4,184,128]{2,1,0:T(8,128)S(1)} %all_to_all.23.mine), channel_id=1, source_target_pairs={{0,64},{64,0},{128,192},{192,128},{256,320},{320,256},{384,448},{4... | collective-permute-start | bytes 1130504 | tf_op jit(solution)/shard_map/ppermute | solution.py:415

commit v3 on v2

--- a/solution.py
+++ b/solution.py
@@ -7,7 +7,7 @@
 from jax.experimental.pallas import tpu as pltpu
 from jax.sharding import PartitionSpec as P
 
-F32 = jnp.float32
+F32, BF = jnp.float32, jnp.bfloat16
 HI = lax.Precision.HIGHEST
 NV = 128
 NC = 2048
@@ -28,6 +28,15 @@
 
 def dot_tn(a, b):
     return lax.dot_general(a, b, (((0,), (0,)), ((), ())), precision=HI, preferred_element_type=F32)
+
+
+def dot_bf(a, b):
+    return lax.dot_general(a, b, (((1,), (0,)), ((), ())), preferred_element_type=F32)
+
+
+def split(x):
+    hi = x.astype(BF)
+    return hi, (x - hi.astype(F32)).astype(BF)
 
 
 def iota(shape, dim):
@@ -114,8 +123,13 @@
     return [a + b for a, b in zip([row[0]] + pairs, pairs + [row[-1]])]
 
 
-def front_kernel(planes, index, left, right, from_left, from_right, w_out, full_out, wg_out, rho_s, both, hot):
+def front_kernel(
+    planes, index, stiff, index_v, left, right, from_left, from_right, w_out, full_out, wg_out, tile_out, rho_s, both, hot
+):
     h = lax.axis_index("halo")
+    tile_out[...] = jnp.zeros((8, NV), F32)
+    tile_out[0:2, 0:16] = stiff[0]
+    tile_out[2:4, 0:16] = (index_v[0] + h * NC).astype(F32)
     lane = iota((8, NV), 1)
     half_lo = jnp.where(lane == 0, 0.0, 0.5).astype(F32)
     half_hi = jnp.where(lane == NV - 1, 0.0, 0.5).astype(F32)
@@ -196,7 +210,7 @@
             hot[part * 8 : part * 8 + 8, k * NV : (k + 1) * NV] = jnp.where(col == lane + k * NV, 1.0, 0.0).astype(dtype)
 
 
-def own_kernel(full, wg, stiff, index, li_out, k_out, message, small):
+def own_kernel(full, wg, small, li_out, k_out, message):
     h = lax.axis_index("halo")
     total = jnp.sum(full[...], axis=0)
     packed, diag = total[:NV, :], total[NV : NV + 1, :]
@@ -209,9 +223,6 @@
     li_out[...] = li
     k_out[...] = k
     rows = dot_nt(wg[...], li)
-    small[...] = jnp.zeros((8, NV), F32)
-    small[0:2, 0:16] = stiff[0]
-    small[2:4, 0:16] = (index[0] + h * NC).astype(F32)
     lane, sub = iota((8, NV), 1), iota((8, NV), 0)
     tile = small[...]
     tile = jnp.where(sub < 4, tile, pltpu.roll(pltpu.roll(tile, NV - 8, 1), 4, 0))
@@ -231,23 +242,30 @@
 
 
 def select_kernel(order, got, out, inverse):
+    odd = lax.axis_index("halo") % 2 == 1
     leaf = lax.axis_index("leaf")
     y, z = leaf // SQ, leaf % SQ
     invert(order, inverse)
     for to in range(SQ):
-        position = order[to * SQ + z]
+        position = order[jnp.where(odd, y * SQ + to, to * SQ + z)]
         for role in range(1, 4):
             source = inverse[position ^ role]
-            @pl.when(source // SQ == y)
-            def _(to=to, role=role, source=source):
-                out[to, (role - 1) * ROWS : role * ROWS, :] = got[source % SQ]
+            row, col = source // SQ, source % SQ
+
+            @pl.when(jnp.where(odd, col == z, row == y))
+            def _(to=to, role=role, at=jnp.where(odd, row, col)):
+                out[to, (role - 1) * ROWS : role * ROWS, :] = got[at]
 
 
 def collect_kernel(order, got, message, out, inverse):
+    odd = lax.axis_index("halo") % 2 == 1
     leaf = lax.axis_index("leaf")
     invert(order, inverse)
     position = order[leaf]
-    parts = [got[inverse[position ^ r] // SQ, (r - 1) * ROWS : r * ROWS, :] for r in range(1, 4)]
+    parts = []
+    for r in range(1, 4):
+        source = inverse[position ^ r]
+        parts.append(got[jnp.where(odd, source % SQ, source // SQ), (r - 1) * ROWS : r * ROWS, :])
     own = message[0, 8:, :]
     for peer in range(4):
         for r in range(3):
@@ -292,30 +310,37 @@
             kmat[role] = jnp.where(row <= col, raw, raw.T)
 
     def meet(slot, first, ka, ra, kb, rb, stiff):
-        zero = jnp.zeros((NV, NV), F32)
         ra, rb = scale * ra, scale * rb
         r1, r2 = jnp.where(first, ra, rb), jnp.where(first, rb, ra)
         big[slot, :NV, :NV] = jnp.where(first, ka, kb)
-        big[slot, :NV, NV : 2 * NV] = zero
-        big[slot, :NV, 2 * NV :] = r1.T
-        big[slot, NV : 2 * NV, :NV] = zero
-        big[slot, NV : 2 * NV, NV : 2 * NV] = jnp.where(first, kb, ka)
-        big[slot, NV : 2 * NV, 2 * NV :] = r2.T
+        big[slot, :NV, NV:] = r1.T
+        big[slot, NV : 2 * NV, :NV] = jnp.where(first, kb, ka)
+        big[slot, NV : 2 * NV, NV:] = r2.T
         big[slot, 2 * NV :, :NV] = r1
-        big[slot, 2 * NV :, NV : 2 * NV] = r2
-        big[slot, 2 * NV :, 2 * NV :] = jnp.where(eye, stiff, 0.0)
-
-    def reduce(slots):
-        ys = [dot_nn(big[i], dot_nn(big[i], start[...])) for i in slots]
+        big[slot, 2 * NV :, NV:] = r2
+        return jnp.sum(jnp.where(eye, stiff, 0.0), axis=1, keepdims=True)
+
+    def product(slot, diag, x):
+        x1, x2, x3 = x[:NV], x[NV : 2 * NV], x[2 * NV :]
+        y1 = dot_nn(big[slot, :NV], jnp.concatenate([x1, x3], axis=0))
+        y2 = dot_nn(big[slot, NV : 2 * NV], jnp.concatenate([x2, x3], axis=0))
+        y3 = dot_nn(big[slot, 2 * NV :], x[: 2 * NV]) + diag * x3
+        return jnp.concatenate([y1, y2, y3], axis=0)
+
+    def reduce(diags):
+        ys = [product(i, d, start[...]) for i, d in enumerate(diags)]
+        ys = [product(i, d, y) for i, (d, y) in enumerate(zip(diags, ys))]
         ps = chol_inv([dot_tn(y, y) for y in ys])
-        images = [dot_tn(y, dot_nn(big[i], y)) for i, y in zip(slots, ys)]
+        images = [dot_tn(y, product(i, d, y)) for i, (d, y) in enumerate(zip(diags, ys))]
         return [dot_nt(y, p) for y, p in zip(ys, ps)], [dot_nt(dot_nn(p, im), p) for p, im in zip(ps, images)]
 
     firsts = [ids[0] < ids[1], ids[2] < ids[3]]
+    diags = []
     for pair in range(2):
         a, b = 2 * pair, 2 * pair + 1
-        meet(pair, firsts[pair], kmat[a], rmat[0, a], kmat[b], rmat[0, b], small[a][0:1] + small[b][0:1])
-    zs, ks = reduce([0, 1])
+        diag = meet(pair, firsts[pair], kmat[a], rmat[0, a], kmat[b], rmat[0, b], small[a][0:1] + small[b][0:1])
+        diags.append(diag)
+    zs, ks = reduce(diags)
     joint = []
     for pair in range(2):
         z = zs[pair]
@@ -333,8 +358,8 @@
             z_s[NV:, :] = zi
     first = jnp.minimum(ids[0], ids[1]) < jnp.minimum(ids[2], ids[3])
     stiff = small[0][1:2] + small[1][1:2] + small[2][1:2] + small[3][1:2]
-    meet(0, first, ks[0], joint[0], ks[1], joint[1], stiff)
-    (z1,), (k1,) = reduce([0])
+    diag = meet(0, first, ks[0], joint[0], ks[1], joint[1], stiff)
+    (z1,), (k1,) = reduce([diag])
     reduced_out[...] = k1
     top = jnp.where(first, z1[:NV], z1[NV : 2 * NV])
     at = pl.ds(pl.multiple_of(NV + h * 16, 16), 16)
@@ -345,16 +370,24 @@
     final = math.sqrt(NC * 8)
     mixed = final * dot_tn(top, dot_tn(z_low, li[...]))
     spread = jnp.concatenate([math.sqrt(0.5) * final * dot_nn(low_part, top), 0.5 * final * top_part], axis=0)
-    fill_hot(index, hot, F32)
-    for k in range(16):
-        at = slice(k * NV, (k + 1) * NV)
-        part = dot_nn(mixed, w[:, at]) + dot_tn(spread, hot[:, at])
-        modes_out[pl.ds(k, NV, stride=16), :] = part
+    fill_hot(index, hot, BF)
+    l_hi, l_lo = split(jnp.concatenate([mixed, spread.T], axis=1))
+    for k in range(0, 16, 2):
+        at = slice(k * NV, (k + 2) * NV)
+        r_hi, r_lo = split(w[:, at])
+        tail = jnp.concatenate([r_hi, hot[:, at]], axis=0)
+        part = dot_bf(l_lo, tail) + dot_bf(l_hi[:, :NV], r_lo) + dot_bf(l_hi, tail)
+        modes_out[pl.ds(k, NV, stride=16), :] = part[:, :NV]
+        modes_out[pl.ds(k + 1, NV, stride=16), :] = part[:, NV:]
 
 
 def per_device(start_modes, density, planes, tree_order, iface_index, iface_stiff, reduced_start):
-    row_groups = [[y * SQ + z for z in range(SQ)] for y in range(SQ)]
-    col_groups = [[y * SQ + z for y in range(SQ)] for z in range(SQ)]
+    rows = [[h * 64 + y * SQ + z for z in range(SQ)] for h in range(8) for y in range(SQ)]
+    cols = [[h * 64 + y * SQ + z for y in range(SQ)] for h in range(8) for z in range(SQ)]
+    even = [h % 2 == 0 for h in range(8) for _ in range(SQ)]
+    first_groups = [r if e else c for e, r, c in zip(even, rows, cols)]
+    second_groups = [c if e else r for e, r, c in zip(even, rows, cols)]
+    everyone = ("halo", "leaf")
     chips = [[0, 2, 4, 6], [1, 3, 5, 7]]
     edge = 12 * NV + 16
     left, right = pl.pallas_call(
@@ -368,11 +401,11 @@
     )(planes, start_modes.reshape(NC, NV), density.reshape(16, NV))
     from_left = lax.ppermute(right, "halo", [(i, i + 1) for i in range(7)])
     from_right = lax.ppermute(left, "halo", [(i + 1, i) for i in range(7)])
-    w, full, wg = pl.pallas_call(
+    w, full, wg, small = pl.pallas_call(
         front_kernel,
-        out_shape=(shape(NV, NC), shape(8, NV + 8, NV), shape(32, NV)),
-        in_specs=[SM, SM, VM, VM, VM, VM],
-        out_specs=(VM, VM, VM),
+        out_shape=(shape(NV, NC), shape(8, NV + 8, NV), shape(32, NV), shape(8, NV)),
+        in_specs=[SM, SM, VM, VM, VM, VM, VM, VM],
+        out_specs=(VM, VM, VM, VM),
         scratch_shapes=[
             pltpu.VMEM((10, 4, 8, NV), F32),
             pltpu.VMEM((2 * NV, NC), F32),
@@ -380,18 +413,17 @@
         ],
         name="front",
         compiler_params=grant(24),
-    )(planes, iface_index, left, right, from_left, from_right)
+    )(planes, iface_index, iface_stiff, iface_index, left, right, from_left, from_right)
     full = lax.all_to_all(full, "halo", 0, 0, tiled=True)
     li, k_own, message = pl.pallas_call(
         own_kernel,
         out_shape=(shape(NV, NV), shape(NV, NV), shape(SQ, ROWS, NV)),
-        in_specs=[VM, VM, VM, VM],
+        in_specs=[VM, VM, VM],
         out_specs=(VM, VM, VM),
-        scratch_shapes=[pltpu.VMEM((8, NV), F32)],
         name="own",
         compiler_params=grant(8),
-    )(full, wg, iface_stiff, iface_index)
-    along = lax.all_to_all(message, "leaf", 0, 0, tiled=True, axis_index_groups=row_groups)
+    )(full, wg, small)
+    along = lax.all_to_all(message, everyone, 0, 0, tiled=True, axis_index_groups=first_groups)
     chosen = pl.pallas_call(
         select_kernel,
         out_shape=shape(SQ, 3 * ROWS, NV),
@@ -401,7 +433,7 @@
         name="select",
         compiler_params=grant(4),
     )(tree_order, along)
-    across = lax.all_to_all(chosen, "leaf", 0, 0, tiled=True, axis_index_groups=col_groups)
+    across = lax.all_to_all(chosen, everyone, 0, 0, tiled=True, axis_index_groups=second_groups)
     gathered = pl.pallas_call(
         collect_kernel,
         out_shape=shape(4, AG, NV),
@@ -422,9 +454,9 @@
             pltpu.SMEM((SQ * SQ,), jnp.int32),
             pltpu.VMEM((4, NV, NV), F32),
             pltpu.VMEM((2, 4, NV, NV), F32),
-            pltpu.VMEM((2, 3 * NV, 3 * NV), F32),
+            pltpu.VMEM((2, 3 * NV, 2 * NV), F32),
             pltpu.VMEM((2 * NV, NV), F32),
-            pltpu.VMEM((32, NC), F32),
+            pltpu.VMEM((32, NC), BF),
         ],
         name="solve",
         compiler_params=grant(20),

time: 132 us -> 124 us (0.939)
  blocking collectives: 61.3 us -> 58 us
  Pallas kernels: 38.2 us -> 35.2 us
    all_to_all x2, blocking collectives: 38.6 us -> 35.2 us  [the longest x1 22.7 us: per_device(): lax.all_to_all(chosen, everyone, 0, 0, tiled=True, axis_index_groups=seco...]
    pallas_call x1, Pallas kernels: 20.9 us -> 17.8 us  [per_device(): pl.pallas_call(solve_kernel, out_shape=(shape(NC, NV), shape(NV, NV)), in...]
where the time goes in v3:
time: 124 us
  blocking collectives  58 us (47%)
  Pallas kernels  35.2 us (28%)
  starting transfers between devices  17.3 us (14%)
  waiting for transfers between devices  10.1 us (8%)
  local copies, waits for them, and re-layouts  1.76 us (1%)
  between operations  1.38 us (1%)
    all_to_all x1, blocking collectives, per_device(): lax.all_to_all(chosen, everyone, 0, 0, tiled=True, axis_index_groups=seco...  22.7 us
    pallas_call x1, Pallas kernels, per_device(): pl.pallas_call(solve_kernel, out_shape=(shape(NC, NV), shape(NV, NV)), in...  17.8 us
    all_to_all x1, blocking collectives, per_device(): full = lax.all_to_all(full, 'halo', 0, 0, tiled=True)  14.1 us
    all_to_all x1, blocking collectives, per_device(): lax.all_to_all(message, everyone, 0, 0, tiled=True, axis_index_groups=fir...  12.5 us
    pallas_call x1, Pallas kernels, per_device(): pl.pallas_call(front_kernel, out_shape=(shape(NV, NC), shape(8, NV + 8, N...  10.4 us
    ppermute x1, starting transfers between devices, per_device(): from_right = lax.ppermute(left, 'halo', [(i + 1, i) for i in range(7)])  8.75 us
    all_to_all x1, blocking collectives, per_device(): lax.all_to_all(gathered, 'halo', 0, 0, tiled=True, axis_index_groups=chips)  8.66 us
    ppermute x1, starting transfers between devices, per_device(): other = lax.ppermute(mine, 'halo', [(i, i ^ 1) for i in range(8)])  6.66 us
  transfers between devices with their start and end apart: 3, of which 3 were waited for; matrix products, arithmetic and copies ran while one was open for 0% of the time, Pallas kernels for 0%

profile of v3, /device:TPU:1, one launch (start us, length us, event | category | flops | bytes accessed | tf_op | source)
XLA Modules:
  0.0 123.8 jit_solution(10659371681330544336)
XLA Ops:
  1.3 0.0 copy-start
  1.3 1.0 copy-done
  2.3 0.0 copy-start.3
  2.3 0.7 copy-done.3
  3.0 0.5 prep.1
  3.5 0.0 copy-start.5
  3.6 0.0 copy-start.2
  3.6 8.7 %collective-permute-start.1 = (f32[1552,128]{1,0:T(8,128)S(1)}, f32[1552,128]{1,0:T(8,128)S(1)}, u32[]{:S(2)}, u32[]{:S(2)}) collective-permute-start(f32[1552,128]{1,0:T(8,128)S(1)} %get-tuple-element.13.left), channel_id=1, source_target_pairs={{64,0},{128,64},{192,128},{256,192},{320,256},{384,320},{448,384},... | collective-permute-start | bytes 2383880 | tf_op jit(solution)/shard_map/ppermute | solution.py:403
  12.3 1.9 %collective-permute-start = (f32[1552,128]{1,0:T(8,128)S(1)}, f32[1552,128]{1,0:T(8,128)S(1)}, u32[]{:S(2)}, u32[]{:S(2)}) collective-permute-start(f32[1552,128]{1,0:T(8,128)S(1)} %get-tuple-element.14.right), channel_id=1, source_target_pairs={{0,64},{64,128},{128,192},{192,256},{256,320},{320,384},{384,448},... | collective-permute-start | bytes 2383880 | tf_op jit(solution)/shard_map/ppermute | solution.py:402
  14.3 3.6 %collective-permute-done.1.from_right = f32[1552,128]{1,0:T(8,128)S(1)} collective-permute-done((f32[1552,128]{1,0:T(8,128)S(1)}, f32[1552,128]{1,0:T(8,128)S(1)}, u32[]{:S(2)}, u32[]{:S(2)}) %collective-permute-start.1) | collective-permute-done | bytes 794656 | tf_op jit(solution)/shard_map/ppermute | solution.py:403
  17.8 5.4 %collective-permute-done.from_left = f32[1552,128]{1,0:T(8,128)S(1)} collective-permute-done((f32[1552,128]{1,0:T(8,128)S(1)}, f32[1552,128]{1,0:T(8,128)S(1)}, u32[]{:S(2)}, u32[]{:S(2)}) %collective-permute-start) | collective-permute-done | bytes 794656 | tf_op jit(solution)/shard_map/ppermute | solution.py:402
  23.3 0.0 copy-done.5
  23.3 0.0 copy-done.2
  23.3 10.4 %front.1 = (f32[128,2048]{1,0:T(8,128)S(1)}, f32[8,136,128]{2,1,0:T(8,128)S(1)}, f32[32,128]{1,0:T(8,128)S(1)}, f32[8,128]{1,0:T(8,128)S(1)}) custom-call(s32[1]{0:T(128)S(6)} %copy.9.planes, s32[1,2,16]{2,1,0:T(2,128)S(1)} %copy-done.2, f32[1,2,16]{2,1,0:T(2,128)S(1)} %copy-done.5, s32[1,2,16]{2,1,0:T(2,128)S(1)} %copy-done.2, ...), custom_call_target="tpu_custom_call" | custom-call | tf_op jit(solution)/shard_map/front/pallas_call | solution.py:404
  33.7 14.1 %all_to_all.20.full = f32[8,136,128]{2,1,0:T(8,128)S(1)} all-to-all(f32[8,136,128]{2,1,0:T(8,128)S(1)} %get-tuple-element.15), channel_id=1, replica_groups=mesh['halo'=8,'leaf'=64] {'halo'}, dimensions={0} | all-to-all | bytes 1114112 | tf_op jit(solution)/shard_map/all_to_all | solution.py:417
  47.8 4.7 %own.1 = (f32[128,128]{1,0:T(8,128)S(1)}, f32[128,128]{1,0:T(8,128)S(1)}, f32[8,48,128]{2,1,0:T(8,128)S(1)}) custom-call(f32[8,136,128]{2,1,0:T(8,128)S(1)} %all_to_all.20.full, f32[32,128]{1,0:T(8,128)S(1)} %get-tuple-element.16.wg, f32[8,128]{1,0:T(8,128)S(1)} %get-tuple-element.17.small), custom_call_target="tpu_custom_call" | custom-call | tf_op jit(solution)/shard_map/own/pallas_call | solution.py:418
  52.5 0.0 copy-start.4
  52.5 12.5 %all_to_all.21.got = f32[8,48,128]{2,1,0:T(8,128)S(1)} all-to-all(f32[8,48,128]{2,1,0:T(8,128)S(1)} %get-tuple-element.18.message), channel_id=1, replica_groups={{0,1,2,3,4,5,6,7},{8,9,10,11,12,13,14,15},{16,17,18,19,20,21,22,23},{24..., dimensions={0} | all-to-all | bytes 393216 | tf_op jit(solution)/shard_map/all_to_all | solution.py:426
  65.0 0.0 copy-done.4
  65.1 1.1 select.1
  66.1 22.7 %all_to_all.22.got = f32[8,144,128]{2,1,0:T(8,128)S(1)} all-to-all(f32[8,144,128]{2,1,0:T(8,128)S(1)} %select.1), channel_id=1, replica_groups={{0,8,16,24,32,40,48,56},{1,9,17,25,33,41,49,57},{2,10,18,26,34,42,50,58..., dimensions={0} | all-to-all | bytes 1179648 | tf_op jit(solution)/shard_map/all_to_all | solution.py:436
  88.8 0.6 collect.1
  89.5 0.0 copy-start.1
  89.5 8.7 %all_to_all.23.mine = f32[4,184,128]{2,1,0:T(8,128)S(1)} all-to-all(f32[4,184,128]{2,1,0:T(8,128)S(1)} %collect.1), channel_id=1, replica_groups={{0,128,256,384},{64,192,320,448},{1,129,257,385},{65,193,321,449},{2,13..., dimensions={0} | all-to-all | bytes 753664 | tf_op jit(solution)/shard_map/all_to_all | solution.py:446
  98.1 6.7 %collective-permute-start.2 = (f32[4,184,128]{2,1,0:T(8,128)S(1)}, f32[4,184,128]{2,1,0:T(8,128)S(1)}, u32[]{:S(2)}, u32[]{:S(2)}) collective-permute-start(f32[4,184,128]{2,1,0:T(8,128)S(1)} %all_to_all.23.mine), channel_id=1, source_target_pairs={{0,64},{64,0},{128,192},{192,128},{256,320},{320,256},{384,448},{4... | collective-permute-start | bytes 1130504 | tf_op jit(solution)/shard_map/ppermute | solution.py:447
  104.8 1.1 collective-permute-done.2.other
  105.9 0.0 copy-done.1
  105.9 17.8 %solve.1 = (f32[2048,128]{1,0:T(8,128)}, f32[128,128]{1,0:T(8,128)}) custom-call(s32[64]{0:T(128)S(1)} %copy-done.4, s32[1,2,16]{2,1,0:T(2,128)S(1)} %copy-done.2, f32[4,184,128]{2,1,0:T(8,128)S(1)} %all_to_all.23.mine, f32[4,184,128]{2,1,0:T(8,128)S(1)} %collective-permute-done.2.other, f32[128,128]{1,0:T(8,128)S(1)} %get-tuple-element.19.k_own, ...), custom_call_target="tpu_custom_call" | custom-call | tf_op jit(solution)/shard_map/solve/pallas_call | solution.py:448
Async XLA Ops:
  1.3 1.0 copy-start
  2.3 0.7 copy-start.3
  3.5 19.7 %copy-start.5 = (f32[1,2,16]{2,1,0:T(2,128)S(1)}, f32[1,2,16]{2,1,0:T(2,128)}, u32[]{:S(2)}) copy-start(f32[1,2,16]{2,1,0:T(2,128)} %stiff.1) | copy-start | bytes 388
  3.6 19.7 %copy-start.2 = (s32[1,2,16]{2,1,0:T(2,128)S(1)}, s32[1,2,16]{2,1,0:T(2,128)}, u32[]{:S(2)}) copy-start(s32[1,2,16]{2,1,0:T(2,128)} %index.3) | copy-start | bytes 388
  3.6 14.3 %collective-permute-start.1 = (f32[1552,128]{1,0:T(8,128)S(1)}, f32[1552,128]{1,0:T(8,128)S(1)}, u32[]{:S(2)}, u32[]{:S(2)}) collective-permute-start(f32[1552,128]{1,0:T(8,128)S(1)} %get-tuple-element.13.left), channel_id=1, source_target_pairs={{64,0},{128,64},{192,128},{256,192},{320,256},{384,320},{448,384},... | collective-permute-start | bytes 2383880 | tf_op jit(solution)/shard_map/ppermute | solution.py:403
  12.3 10.9 %collective-permute-start = (f32[1552,128]{1,0:T(8,128)S(1)}, f32[1552,128]{1,0:T(8,128)S(1)}, u32[]{:S(2)}, u32[]{:S(2)}) collective-permute-start(f32[1552,128]{1,0:T(8,128)S(1)} %get-tuple-element.14.right), channel_id=1, source_target_pairs={{0,64},{64,128},{128,192},{192,256},{256,320},{320,384},{384,448},... | collective-permute-start | bytes 2383880 | tf_op jit(solution)/shard_map/ppermute | solution.py:402
  52.5 12.5 %copy-start.4 = (s32[64]{0:T(128)S(1)}, s32[64]{0:T(128)}, u32[]{:S(2)}) copy-start(s32[64]{0:T(128)} %order.5) | copy-start | bytes 772
  89.5 16.5 %copy-start.1 = (f32[384,128]{1,0:T(8,128)S(1)}, f32[384,128]{1,0:T(8,128)}, u32[]{:S(2)}) copy-start(f32[384,128]{1,0:T(8,128)} %start.1) | copy-start | bytes 589828
  98.1 7.8 %collective-permute-start.2 = (f32[4,184,128]{2,1,0:T(8,128)S(1)}, f32[4,184,128]{2,1,0:T(8,128)S(1)}, u32[]{:S(2)}, u32[]{:S(2)}) collective-permute-start(f32[4,184,128]{2,1,0:T(8,128)S(1)} %all_to_all.23.mine), channel_id=1, source_target_pairs={{0,64},{64,0},{128,192},{192,128},{256,320},{320,256},{384,448},{4... | collective-permute-start | bytes 1130504 | tf_op jit(solution)/shard_map/ppermute | solution.py:447

commit v4 on v3

--- a/solution.py
+++ b/solution.py
@@ -16,6 +16,7 @@
 AG = 3 * ROWS + 40
 VM = pl.BlockSpec(memory_space=pltpu.VMEM)
 SM = pl.BlockSpec(memory_space=pltpu.SMEM)
+FAR = pl.BlockSpec(memory_space=pltpu.HBM)
 
 
 def dot_nt(a, b):
@@ -43,6 +44,10 @@
     return lax.broadcasted_iota(jnp.int32, shape, dim)
 
 
+def far(x):
+    return pltpu.with_memory_space_constraint(x, pltpu.HBM)
+
+
 def grant(mib):
     return pltpu.CompilerParams(vmem_limit_bytes=mib << 20)
 
@@ -51,9 +56,10 @@
     return jax.ShapeDtypeStruct(dims, F32)
 
 
-def chol_inv(mats):
-    count = len(mats)
-    sh = (count, 8, NV)
+def eliminate(mats):
+    count, width = len(mats), mats[0].shape[1]
+    n = width // 8
+    sh = (count, 8, width)
     lane, sub = iota(sh, 2), iota(sh, 1)
 
     def over_lanes(x, c):
@@ -62,30 +68,45 @@
     def over_subs(x, r):
         return jnp.broadcast_to(x[:, r : r + 1, :], sh)
 
-    rows = [jnp.stack([m[8 * i : 8 * i + 8, :] for m in mats]) for i in range(16)]
-    for s in range(16):
-        p = rows[s]
-        cols = [over_lanes(p, 8 * s + j) for j in range(8)]
-        scaled, scales, upper = [], [], {}
+    rows = [jnp.stack([m[8 * i : 8 * i + 8, :] for m in mats]) for i in range(n)]
+    ready = [over_lanes(rows[0], j) for j in range(8)]
+    for s in range(n):
+        p, cols = rows[s], ready
+        inside = (lane >= 8 * s) & (lane < 8 * s + 8)
+        after = s + 1 < n
+        if after:
+            q = rows[s + 1]
+            mine = [over_lanes(q, 8 * s + j) for j in range(8)]
+            ready = [over_lanes(q, 8 * s + 8 + j) for j in range(8)]
+            q = jnp.where(inside, 0.0, q)
+        scaled, kept, scales, upper = [], [], [], {}
         for k in range(8):
             rs = lax.rsqrt(over_subs(cols[k], k))
             at = lane == 8 * s + k
             r = jnp.where(at, rs, over_subs(p, k) * rs)
             scaled.append(r)
             scales.append(rs)
+            kept.append(jnp.where(inside & (lane > 8 * s + k), 0.0, r))
             if k < 7:
                 low = cols[k] * rs
-                p = jnp.where(sub > k, jnp.where(at, 0.0, p) - low * r, p)
                 for j in range(k + 1, 8):
                     upper[k, j] = over_subs(cols[j], k) * rs
                     cols[j] = cols[j] - low * upper[k, j]
+                p = jnp.where(sub > k, jnp.where(at, 0.0, p) - low * r, p)
+            if after:
+                low = mine[k] * rs
+                for j in range(k + 1, 8):
+                    mine[j] = mine[j] - low * upper[k, j]
+                for j in range(8):
+                    ready[j] = ready[j] - low * over_subs(low, j)
+                q = q - low * kept[k]
         out = scaled[7]
         for k in range(7):
             out = jnp.where(sub == k, scaled[k], out)
         rows[s] = jnp.where(lane > 8 * s + sub, 0.0, out)
-        inside = (lane >= 8 * s) & (lane < 8 * s + 8)
-        kept = [jnp.where(inside & (lane > 8 * s + k), 0.0, scaled[k]) for k in range(8)]
-        for a in range(s + 1, 16):
+        if after:
+            rows[s + 1] = q
+        for a in range(s + 2, n):
             q = rows[a]
             cols = [over_lanes(q, 8 * s + j) for j in range(8)]
             q = jnp.where(inside, 0.0, q)
@@ -95,19 +116,46 @@
                 for j in range(k + 1, 8):
                     cols[j] = cols[j] - low * upper[k, j]
             rows[a] = q
-    return [jnp.concatenate([rows[i][b] for i in range(16)], axis=0) for b in range(count)]
-
-
-def prep_kernel(planes, v, rho, left, right, wide):
+    return [jnp.concatenate([rows[i][b] for i in range(n)], axis=0) for b in range(count)]
+
+
+def chol_inv(mats):
+    if len(mats) == 1:
+        return eliminate(mats)
+    half = NV // 2
+    tops = eliminate([m[:half, :half] for m in mats])
+    sides = [dot_nt(m[half:, :half], t) for m, t in zip(mats, tops)]
+    ends = eliminate([m[half:, half:] - dot_nt(x, x) for m, x in zip(mats, sides)])
+    lows = [dot_nn(e, dot_nn(x, t)) for x, t, e in zip(sides, tops, ends)]
+    zero = jnp.zeros((half, half), F32)
+    return [
+        jnp.concatenate([jnp.concatenate([t, zero], axis=1), jnp.concatenate([-x, e], axis=1)], axis=0)
+        for t, x, e in zip(tops, lows, ends)
+    ]
+
+
+def prep_kernel(planes, v_far, rho_far, left, right, v, wide, rho, sems):
     h = lax.axis_index("halo")
-    wide[...] = v[...].astype(F32)
-    for k in range(16):
-        part = wide[pl.ds(k, NV, stride=16), :]
-        part = jnp.where(h * 4 + k // 4 < planes[0], part, 0.0)
-        if k < 12:
-            left[k * NV : (k + 1) * NV, :] = part
-        if k >= 4:
-            right[(k - 4) * NV : (k - 3) * NV, :] = part
+    step = NC // 4
+    copies = [
+        pltpu.make_async_copy(v_far.at[i * step : (i + 1) * step], v.at[i * step : (i + 1) * step], sems.at[i])
+        for i in range(4)
+    ]
+    copies.append(pltpu.make_async_copy(rho_far, rho, sems.at[4]))
+    for copy in copies:
+        copy.start()
+    for i in range(4):
+        copies[i].wait()
+        wide[i * step : (i + 1) * step, :] = v[i * step : (i + 1) * step, :].astype(F32)
+        for k in range(16):
+            part = wide[pl.ds(i * step + k, NV // 4, stride=16), :]
+            part = jnp.where(h * 4 + k // 4 < planes[0], part, 0.0)
+            at = k * NV + i * (NV // 4)
+            if k < 12:
+                left[at : at + NV // 4, :] = part
+            if k >= 4:
+                right[at - 4 * NV : at - 4 * NV + NV // 4, :] = part
+    copies[4].wait()
     left[12 * NV :, :] = rho[...]
     right[12 * NV : 12 * NV + 12, :] = rho[4:, :]
     right[12 * NV + 12 :, :] = rho[:4, :]
@@ -124,7 +172,7 @@
 
 
 def front_kernel(
-    planes, index, stiff, index_v, left, right, from_left, from_right, w_out, full_out, wg_out, tile_out, rho_s, both, hot
+    planes, index, stiff, index_v, left, right, from_left, from_right, w_out, full_out, wg_out, tile_out, rho_s, both, acc
 ):
     h = lax.axis_index("halo")
     tile_out[...] = jnp.zeros((8, NV), F32)
@@ -171,13 +219,13 @@
             ref, p = place(q)
             cells.append([ref[pl.ds(pl.multiple_of((4 * p + c) * NV + g * 8, 8), 8), :] for c in range(4)])
         cells = apply(apply(cells, 0), 1)
-        rows = pl.ds(pl.multiple_of(g * 8, 8), 8)
+        rows = pl.ds(pl.multiple_of(32 + g * 8, 8), 8)
         for p in range(4):
             for c in range(4):
                 k = 4 * p + c
                 both[rows, k * NV : (k + 1) * NV] = cells[p + 1][c]
         cells = apply(cells, 2)
-        rows = pl.ds(pl.multiple_of(NV + g * 8, 8), 8)
+        rows = pl.ds(pl.multiple_of(32 + NV + g * 8, 8), 8)
         for p in range(4):
             for c in range(4):
                 k = 4 * p + c
@@ -185,13 +233,19 @@
         return carry
 
     lax.fori_loop(0, NV // 8, group, 0)
-    fill_hot(index, hot, F32)
-    w = both[:NV, :]
-    w_out[...] = w
-    gram = dot_nt(w, both[...])
-    wg_out[...] = dot_nt(hot[...], w)
+    fill_hot(index, both, F32)
+    w_out[...] = both[32 : 32 + NV, :]
+    acc[...] = jnp.zeros((32 + NV, 2 * NV), F32)
+
+    def chunk(i, carry):
+        at = pl.ds(pl.multiple_of(i * 256, 256), 256)
+        acc[...] += dot_nt(both[: 32 + NV, at], both[32:, at])
+        return carry
+
+    lax.fori_loop(0, NC // 256, chunk, 0)
+    wg_out[...] = acc[:32, :NV]
     row, col = iota((NV, NV), 0), iota((NV, NV), 1)
-    s, c = gram[:, :NV], gram[:, NV:]
+    s, c = acc[32:, :NV], acc[32:, NV:]
     packed = jnp.where(row >= col, s, c)
     diag = jnp.sum(jnp.where(row == col, c, 0.0), axis=0, keepdims=True)
     for peer in range(8):
@@ -393,12 +447,17 @@
     left, right = pl.pallas_call(
         prep_kernel,
         out_shape=(shape(edge, NV), shape(edge, NV)),
-        in_specs=[SM, VM, VM],
+        in_specs=[SM, FAR, FAR],
         out_specs=(VM, VM),
-        scratch_shapes=[pltpu.VMEM((NC, NV), F32)],
+        scratch_shapes=[
+            pltpu.VMEM((NC, NV), BF),
+            pltpu.VMEM((NC, NV), F32),
+            pltpu.VMEM((16, NV), F32),
+            pltpu.SemaphoreType.DMA((5,)),
+        ],
         name="prep",
         compiler_params=grant(8),
-    )(planes, start_modes.reshape(NC, NV), density.reshape(16, NV))
+    )(planes, far(start_modes.reshape(NC, NV)), far(density.reshape(16, NV)))
     from_left = lax.ppermute(right, "halo", [(i, i + 1) for i in range(7)])
     from_right = lax.ppermute(left, "halo", [(i + 1, i) for i in range(7)])
     w, full, wg, small = pl.pallas_call(
@@ -408,8 +467,8 @@
         out_specs=(VM, VM, VM, VM),
         scratch_shapes=[
             pltpu.VMEM((10, 4, 8, NV), F32),
-            pltpu.VMEM((2 * NV, NC), F32),
-            pltpu.VMEM((32, NC), F32),
+            pltpu.VMEM((32 + 2 * NV, NC), F32),
+            pltpu.VMEM((32 + NV, 2 * NV), F32),
         ],
         name="front",
         compiler_params=grant(24),

time: 124 us -> 120 us (0.968)
  Pallas kernels: 35.2 us -> 33 us
  local copies, waits for them, and re-layouts: 1.76 us -> 0.03 us
    pallas_call x1, Pallas kernels: 17.8 us -> 15.3 us  [per_device(): pl.pallas_call(solve_kernel, out_shape=(shape(NC, NV), shape(NV, NV)), in...]
    unnamed x12 -> x8, local copies, waits for them, and re-layouts: 1.76 us -> 0.03 us
where the time goes in v4:
time: 120 us
  blocking collectives  58 us (48%)
  Pallas kernels  33 us (28%)
  starting transfers between devices  17.3 us (14%)
  waiting for transfers between devices  10.1 us (8%)
  between operations  1.38 us (1%)
    all_to_all x1, blocking collectives, per_device(): lax.all_to_all(chosen, everyone, 0, 0, tiled=True, axis_index_groups=seco...  22.7 us
    pallas_call x1, Pallas kernels, per_device(): pl.pallas_call(solve_kernel, out_shape=(shape(NC, NV), shape(NV, NV)), in...  15.3 us
    all_to_all x1, blocking collectives, per_device(): full = lax.all_to_all(full, 'halo', 0, 0, tiled=True)  14.1 us
    all_to_all x1, blocking collectives, per_device(): lax.all_to_all(message, everyone, 0, 0, tiled=True, axis_index_groups=fir...  12.5 us
    pallas_call x1, Pallas kernels, per_device(): pl.pallas_call(front_kernel, out_shape=(shape(NV, NC), shape(8, NV + 8, N...  10.9 us
    ppermute x1, starting transfers between devices, per_device(): from_right = lax.ppermute(left, 'halo', [(i + 1, i) for i in range(7)])  8.75 us
    all_to_all x1, blocking collectives, per_device(): lax.all_to_all(gathered, 'halo', 0, 0, tiled=True, axis_index_groups=chips)  8.66 us
    ppermute x1, starting transfers between devices, per_device(): other = lax.ppermute(mine, 'halo', [(i, i ^ 1) for i in range(8)])  6.65 us
  transfers between devices with their start and end apart: 3, of which 3 were waited for; matrix products, arithmetic and copies ran while one was open for 0% of the time, Pallas kernels for 0%

profile of v4, /device:TPU:1, one launch (start us, length us, event | category | flops | bytes accessed | tf_op | source)
XLA Modules:
  0.0 119.8 jit_solution(7608668773216575064)
XLA Ops:
  1.3 1.4 %prep.1 = (f32[1552,128]{1,0:T(8,128)S(1)}, f32[1552,128]{1,0:T(8,128)S(1)}) custom-call(s32[1]{0:T(128)S(6)} %copy.9.planes, bf16[2048,128]{1,0:T(8,128)(2,1)} %bitcast.4, f32[16,128]{1,0:T(8,128)} %bitcast.5), custom_call_target="tpu_custom_call" | custom-call | tf_op jit(solution)/shard_map/prep/pallas_call | solution.py:447
  2.7 0.0 copy-start.3
  2.7 0.0 copy-start.1
  2.7 8.7 %collective-permute-start.1 = (f32[1552,128]{1,0:T(8,128)S(1)}, f32[1552,128]{1,0:T(8,128)S(1)}, u32[]{:S(2)}, u32[]{:S(2)}) collective-permute-start(f32[1552,128]{1,0:T(8,128)S(1)} %get-tuple-element.13.left), channel_id=1, source_target_pairs={{64,0},{128,64},{192,128},{256,192},{320,256},{384,320},{448,384},... | collective-permute-start | bytes 2383880 | tf_op jit(solution)/shard_map/ppermute | solution.py:462
  11.5 1.9 %collective-permute-start = (f32[1552,128]{1,0:T(8,128)S(1)}, f32[1552,128]{1,0:T(8,128)S(1)}, u32[]{:S(2)}, u32[]{:S(2)}) collective-permute-start(f32[1552,128]{1,0:T(8,128)S(1)} %get-tuple-element.14.right), channel_id=1, source_target_pairs={{0,64},{64,128},{128,192},{192,256},{256,320},{320,384},{384,448},... | collective-permute-start | bytes 2383880 | tf_op jit(solution)/shard_map/ppermute | solution.py:461
  13.4 3.6 %collective-permute-done.1.from_right = f32[1552,128]{1,0:T(8,128)S(1)} collective-permute-done((f32[1552,128]{1,0:T(8,128)S(1)}, f32[1552,128]{1,0:T(8,128)S(1)}, u32[]{:S(2)}, u32[]{:S(2)}) %collective-permute-start.1) | collective-permute-done | bytes 794656 | tf_op jit(solution)/shard_map/ppermute | solution.py:462
  17.0 5.4 %collective-permute-done.from_left = f32[1552,128]{1,0:T(8,128)S(1)} collective-permute-done((f32[1552,128]{1,0:T(8,128)S(1)}, f32[1552,128]{1,0:T(8,128)S(1)}, u32[]{:S(2)}, u32[]{:S(2)}) %collective-permute-start) | collective-permute-done | bytes 794656 | tf_op jit(solution)/shard_map/ppermute | solution.py:461
  22.4 0.0 copy-done.3
  22.4 0.0 copy-done.1
  22.4 10.9 %front.1 = (f32[128,2048]{1,0:T(8,128)S(1)}, f32[8,136,128]{2,1,0:T(8,128)S(1)}, f32[32,128]{1,0:T(8,128)S(1)}, f32[8,128]{1,0:T(8,128)S(1)}) custom-call(s32[1]{0:T(128)S(6)} %copy.9.planes, s32[1,2,16]{2,1,0:T(2,128)S(1)} %copy-done.1, f32[1,2,16]{2,1,0:T(2,128)S(1)} %copy-done.3, s32[1,2,16]{2,1,0:T(2,128)S(1)} %copy-done.1, ...), custom_call_target="tpu_custom_call" | custom-call | tf_op jit(solution)/shard_map/front/pallas_call | solution.py:463
  33.3 14.1 %all_to_all.20.full = f32[8,136,128]{2,1,0:T(8,128)S(1)} all-to-all(f32[8,136,128]{2,1,0:T(8,128)S(1)} %get-tuple-element.15), channel_id=1, replica_groups=mesh['halo'=8,'leaf'=64] {'halo'}, dimensions={0} | all-to-all | bytes 1114112 | tf_op jit(solution)/shard_map/all_to_all | solution.py:476
  47.4 3.7 %own.1 = (f32[128,128]{1,0:T(8,128)S(1)}, f32[128,128]{1,0:T(8,128)S(1)}, f32[8,48,128]{2,1,0:T(8,128)S(1)}) custom-call(f32[8,136,128]{2,1,0:T(8,128)S(1)} %all_to_all.20.full, f32[32,128]{1,0:T(8,128)S(1)} %get-tuple-element.16.wg, f32[8,128]{1,0:T(8,128)S(1)} %get-tuple-element.17.small), custom_call_target="tpu_custom_call" | custom-call | tf_op jit(solution)/shard_map/own/pallas_call | solution.py:477
  51.1 0.0 copy-start.2
  51.1 12.5 %all_to_all.21.got = f32[8,48,128]{2,1,0:T(8,128)S(1)} all-to-all(f32[8,48,128]{2,1,0:T(8,128)S(1)} %get-tuple-element.18.message), channel_id=1, replica_groups={{0,1,2,3,4,5,6,7},{8,9,10,11,12,13,14,15},{16,17,18,19,20,21,22,23},{24..., dimensions={0} | all-to-all | bytes 393216 | tf_op jit(solution)/shard_map/all_to_all | solution.py:485
  63.6 0.0 copy-done.2
  63.6 1.1 select.1
  64.7 22.7 %all_to_all.22.got = f32[8,144,128]{2,1,0:T(8,128)S(1)} all-to-all(f32[8,144,128]{2,1,0:T(8,128)S(1)} %select.1), channel_id=1, replica_groups={{0,8,16,24,32,40,48,56},{1,9,17,25,33,41,49,57},{2,10,18,26,34,42,50,58..., dimensions={0} | all-to-all | bytes 1179648 | tf_op jit(solution)/shard_map/all_to_all | solution.py:495
  87.4 0.6 collect.1
  88.0 0.0 copy-start
  88.1 8.7 %all_to_all.23.mine = f32[4,184,128]{2,1,0:T(8,128)S(1)} all-to-all(f32[4,184,128]{2,1,0:T(8,128)S(1)} %collect.1), channel_id=1, replica_groups={{0,128,256,384},{64,192,320,448},{1,129,257,385},{65,193,321,449},{2,13..., dimensions={0} | all-to-all | bytes 753664 | tf_op jit(solution)/shard_map/all_to_all | solution.py:505
  96.7 6.7 %collective-permute-start.2 = (f32[4,184,128]{2,1,0:T(8,128)S(1)}, f32[4,184,128]{2,1,0:T(8,128)S(1)}, u32[]{:S(2)}, u32[]{:S(2)}) collective-permute-start(f32[4,184,128]{2,1,0:T(8,128)S(1)} %all_to_all.23.mine), channel_id=1, source_target_pairs={{0,64},{64,0},{128,192},{192,128},{256,320},{320,256},{384,448},{4... | collective-permute-start | bytes 1130504 | tf_op jit(solution)/shard_map/ppermute | solution.py:506
  103.4 1.1 collective-permute-done.2.other
  104.5 0.0 copy-done
  104.5 15.3 %solve.1 = (f32[2048,128]{1,0:T(8,128)}, f32[128,128]{1,0:T(8,128)}) custom-call(s32[64]{0:T(128)S(1)} %copy-done.2, s32[1,2,16]{2,1,0:T(2,128)S(1)} %copy-done.1, f32[4,184,128]{2,1,0:T(8,128)S(1)} %all_to_all.23.mine, f32[4,184,128]{2,1,0:T(8,128)S(1)} %collective-permute-done.2.other, f32[128,128]{1,0:T(8,128)S(1)} %get-tuple-element.19.k_own, ...), custom_call_target="tpu_custom_call" | custom-call | tf_op jit(solution)/shard_map/solve/pallas_call | solution.py:507
Async XLA Ops:
  2.7 19.7 %copy-start.3 = (f32[1,2,16]{2,1,0:T(2,128)S(1)}, f32[1,2,16]{2,1,0:T(2,128)}, u32[]{:S(2)}) copy-start(f32[1,2,16]{2,1,0:T(2,128)} %stiff.1) | copy-start | bytes 388
  2.7 19.7 %copy-start.1 = (s32[1,2,16]{2,1,0:T(2,128)S(1)}, s32[1,2,16]{2,1,0:T(2,128)}, u32[]{:S(2)}) copy-start(s32[1,2,16]{2,1,0:T(2,128)} %index.3) | copy-start | bytes 388
  2.7 14.3 %collective-permute-start.1 = (f32[1552,128]{1,0:T(8,128)S(1)}, f32[1552,128]{1,0:T(8,128)S(1)}, u32[]{:S(2)}, u32[]{:S(2)}) collective-permute-start(f32[1552,128]{1,0:T(8,128)S(1)} %get-tuple-element.13.left), channel_id=1, source_target_pairs={{64,0},{128,64},{192,128},{256,192},{320,256},{384,320},{448,384},... | collective-permute-start | bytes 2383880 | tf_op jit(solution)/shard_map/ppermute | solution.py:462
  11.5 10.9 %collective-permute-start = (f32[1552,128]{1,0:T(8,128)S(1)}, f32[1552,128]{1,0:T(8,128)S(1)}, u32[]{:S(2)}, u32[]{:S(2)}) collective-permute-start(f32[1552,128]{1,0:T(8,128)S(1)} %get-tuple-element.14.right), channel_id=1, source_target_pairs={{0,64},{64,128},{128,192},{192,256},{256,320},{320,384},{384,448},... | collective-permute-start | bytes 2383880 | tf_op jit(solution)/shard_map/ppermute | solution.py:461
  51.1 12.5 %copy-start.2 = (s32[64]{0:T(128)S(1)}, s32[64]{0:T(128)}, u32[]{:S(2)}) copy-start(s32[64]{0:T(128)} %order.5) | copy-start | bytes 772
  88.0 16.5 %copy-start = (f32[384,128]{1,0:T(8,128)S(1)}, f32[384,128]{1,0:T(8,128)}, u32[]{:S(2)}) copy-start(f32[384,128]{1,0:T(8,128)} %start.1) | copy-start | bytes 589828
  96.7 7.8 %collective-permute-start.2 = (f32[4,184,128]{2,1,0:T(8,128)S(1)}, f32[4,184,128]{2,1,0:T(8,128)S(1)}, u32[]{:S(2)}, u32[]{:S(2)}) collective-permute-start(f32[4,184,128]{2,1,0:T(8,128)S(1)} %all_to_all.23.mine), channel_id=1, source_target_pairs={{0,64},{64,0},{128,192},{192,128},{256,320},{320,256},{384,448},{4... | collective-permute-start | bytes 1130504 | tf_op jit(solution)/shard_map/ppermute | solution.py:506

commit v5 on v4

--- a/solution.py
+++ b/solution.py
@@ -57,18 +57,24 @@
 
 
 def eliminate(mats):
-    count, width = len(mats), mats[0].shape[1]
+    side = len(mats)
+    width = NV // side
     n = width // 8
-    sh = (count, 8, width)
-    lane, sub = iota(sh, 2), iota(sh, 1)
+    sh = (8, NV)
+    lane, sub = iota(sh, 1), iota(sh, 0)
+    base = lane - lane % width
+    lane = lane - base
 
     def over_lanes(x, c):
-        return jnp.broadcast_to(x[:, :, c : c + 1], sh)
+        if side == 1:
+            return jnp.broadcast_to(x[:, c : c + 1], sh)
+        return jnp.take_along_axis(x, base + c, axis=1)
 
     def over_subs(x, r):
-        return jnp.broadcast_to(x[:, r : r + 1, :], sh)
-
-    rows = [jnp.stack([m[8 * i : 8 * i + 8, :] for m in mats]) for i in range(n)]
+        return jnp.broadcast_to(x[r : r + 1, :], sh)
+
+    whole = jnp.concatenate(mats, axis=1) if side > 1 else mats[0]
+    rows = [whole[8 * i : 8 * i + 8, :] for i in range(n)]
     ready = [over_lanes(rows[0], j) for j in range(8)]
     for s in range(n):
         p, cols = rows[s], ready
@@ -116,7 +122,8 @@
                 for j in range(k + 1, 8):
                     cols[j] = cols[j] - low * upper[k, j]
             rows[a] = q
-    return [jnp.concatenate([rows[i][b] for i in range(n)], axis=0) for b in range(count)]
+    whole = jnp.concatenate(rows, axis=0)
+    return [whole[:, width * b : width * (b + 1)] for b in range(side)]
 
 
 def chol_inv(mats):
@@ -172,7 +179,7 @@
 
 
 def front_kernel(
-    planes, index, stiff, index_v, left, right, from_left, from_right, w_out, full_out, wg_out, tile_out, rho_s, both, acc
+    planes, index, stiff, index_v, left, right, from_left, from_right, w_out, full_out, wg_out, tile_out, rho_s, both
 ):
     h = lax.axis_index("halo")
     tile_out[...] = jnp.zeros((8, NV), F32)
@@ -232,20 +239,13 @@
                 both[rows, k * NV : (k + 1) * NV] = cells[p][c]
         return carry
 
-    lax.fori_loop(0, NV // 8, group, 0)
+    lax.fori_loop(0, NV // 8, group, 0, unroll=2)
     fill_hot(index, both, F32)
     w_out[...] = both[32 : 32 + NV, :]
-    acc[...] = jnp.zeros((32 + NV, 2 * NV), F32)
-
-    def chunk(i, carry):
-        at = pl.ds(pl.multiple_of(i * 256, 256), 256)
-        acc[...] += dot_nt(both[: 32 + NV, at], both[32:, at])
-        return carry
-
-    lax.fori_loop(0, NC // 256, chunk, 0)
-    wg_out[...] = acc[:32, :NV]
+    gram = dot_nt(both[: 32 + NV, :], both[32:, :])
+    wg_out[...] = gram[:32, :NV]
     row, col = iota((NV, NV), 0), iota((NV, NV), 1)
-    s, c = acc[32:, :NV], acc[32:, NV:]
+    s, c = gram[32:, :NV], gram[32:, NV:]
     packed = jnp.where(row >= col, s, c)
     diag = jnp.sum(jnp.where(row == col, c, 0.0), axis=0, keepdims=True)
     for peer in range(8):
@@ -468,7 +468,6 @@
         scratch_shapes=[
             pltpu.VMEM((10, 4, 8, NV), F32),
             pltpu.VMEM((32 + 2 * NV, NC), F32),
-            pltpu.VMEM((32 + NV, 2 * NV), F32),
         ],
         name="front",
         compiler_params=grant(24),

time: 120 us -> 117 us (0.975)
  Pallas kernels: 33 us -> 30.3 us
    pallas_call x1, Pallas kernels: 10.9 us -> 8.89 us  [per_device(): pl.pallas_call(front_kernel, out_shape=(shape(NV, NC), shape(8, NV + 8, N...]
where the time goes in v5:
time: 117 us
  blocking collectives  58 us (50%)
  Pallas kernels  30.3 us (26%)
  starting transfers between devices  17.3 us (15%)
  waiting for transfers between devices  10.1 us (9%)
  between operations  1.38 us (1%)
    all_to_all x1, blocking collectives, per_device(): lax.all_to_all(chosen, everyone, 0, 0, tiled=True, axis_index_groups=seco...  22.7 us
    pallas_call x1, Pallas kernels, per_device(): pl.pallas_call(solve_kernel, out_shape=(shape(NC, NV), shape(NV, NV)), in...  14.6 us
    all_to_all x1, blocking collectives, per_device(): full = lax.all_to_all(full, 'halo', 0, 0, tiled=True)  14.1 us
    all_to_all x1, blocking collectives, per_device(): lax.all_to_all(message, everyone, 0, 0, tiled=True, axis_index_groups=fir...  12.5 us
    pallas_call x1, Pallas kernels, per_device(): pl.pallas_call(front_kernel, out_shape=(shape(NV, NC), shape(8, NV + 8, N...  8.89 us
    ppermute x1, starting transfers between devices, per_device(): from_right = lax.ppermute(left, 'halo', [(i + 1, i) for i in range(7)])  8.75 us
    all_to_all x1, blocking collectives, per_device(): lax.all_to_all(gathered, 'halo', 0, 0, tiled=True, axis_index_groups=chips)  8.66 us
    ppermute x1, starting transfers between devices, per_device(): other = lax.ppermute(mine, 'halo', [(i, i ^ 1) for i in range(8)])  6.66 us
  transfers between devices with their start and end apart: 3, of which 3 were waited for; matrix products, arithmetic and copies ran while one was open for 0% of the time, Pallas kernels for 0%

profile of v5, /device:TPU:1, one launch (start us, length us, event | category | flops | bytes accessed | tf_op | source)
XLA Modules:
  0.0 117.1 jit_solution(9656744120539232485)
XLA Ops:
  1.3 1.4 %prep.1 = (f32[1552,128]{1,0:T(8,128)S(1)}, f32[1552,128]{1,0:T(8,128)S(1)}) custom-call(s32[1]{0:T(128)S(6)} %copy.9.planes, bf16[2048,128]{1,0:T(8,128)(2,1)} %bitcast.4, f32[16,128]{1,0:T(8,128)} %bitcast.5), custom_call_target="tpu_custom_call" | custom-call | tf_op jit(solution)/shard_map/prep/pallas_call | solution.py:447
  2.7 0.0 copy-start.3
  2.7 0.0 copy-start.1
  2.7 8.7 %collective-permute-start.1 = (f32[1552,128]{1,0:T(8,128)S(1)}, f32[1552,128]{1,0:T(8,128)S(1)}, u32[]{:S(2)}, u32[]{:S(2)}) collective-permute-start(f32[1552,128]{1,0:T(8,128)S(1)} %get-tuple-element.13.left), channel_id=1, source_target_pairs={{64,0},{128,64},{192,128},{256,192},{320,256},{384,320},{448,384},... | collective-permute-start | bytes 2383880 | tf_op jit(solution)/shard_map/ppermute | solution.py:462
  11.5 1.9 %collective-permute-start = (f32[1552,128]{1,0:T(8,128)S(1)}, f32[1552,128]{1,0:T(8,128)S(1)}, u32[]{:S(2)}, u32[]{:S(2)}) collective-permute-start(f32[1552,128]{1,0:T(8,128)S(1)} %get-tuple-element.14.right), channel_id=1, source_target_pairs={{0,64},{64,128},{128,192},{192,256},{256,320},{320,384},{384,448},... | collective-permute-start | bytes 2383880 | tf_op jit(solution)/shard_map/ppermute | solution.py:461
  13.4 3.6 %collective-permute-done.1.from_right = f32[1552,128]{1,0:T(8,128)S(1)} collective-permute-done((f32[1552,128]{1,0:T(8,128)S(1)}, f32[1552,128]{1,0:T(8,128)S(1)}, u32[]{:S(2)}, u32[]{:S(2)}) %collective-permute-start.1) | collective-permute-done | bytes 794656 | tf_op jit(solution)/shard_map/ppermute | solution.py:462
  17.0 5.4 %collective-permute-done.from_left = f32[1552,128]{1,0:T(8,128)S(1)} collective-permute-done((f32[1552,128]{1,0:T(8,128)S(1)}, f32[1552,128]{1,0:T(8,128)S(1)}, u32[]{:S(2)}, u32[]{:S(2)}) %collective-permute-start) | collective-permute-done | bytes 794656 | tf_op jit(solution)/shard_map/ppermute | solution.py:461
  22.4 0.0 copy-done.3
  22.4 0.0 copy-done.1
  22.4 8.9 %front.1 = (f32[128,2048]{1,0:T(8,128)S(1)}, f32[8,136,128]{2,1,0:T(8,128)S(1)}, f32[32,128]{1,0:T(8,128)S(1)}, f32[8,128]{1,0:T(8,128)S(1)}) custom-call(s32[1]{0:T(128)S(6)} %copy.9.planes, s32[1,2,16]{2,1,0:T(2,128)S(1)} %copy-done.1, f32[1,2,16]{2,1,0:T(2,128)S(1)} %copy-done.3, s32[1,2,16]{2,1,0:T(2,128)S(1)} %copy-done.1, ...), custom_call_target="tpu_custom_call" | custom-call | tf_op jit(solution)/shard_map/front/pallas_call | solution.py:463
  31.3 14.1 %all_to_all.20.full = f32[8,136,128]{2,1,0:T(8,128)S(1)} all-to-all(f32[8,136,128]{2,1,0:T(8,128)S(1)} %get-tuple-element.15), channel_id=1, replica_groups=mesh['halo'=8,'leaf'=64] {'halo'}, dimensions={0} | all-to-all | bytes 1114112 | tf_op jit(solution)/shard_map/all_to_all | solution.py:475
  45.4 3.7 %own.1 = (f32[128,128]{1,0:T(8,128)S(1)}, f32[128,128]{1,0:T(8,128)S(1)}, f32[8,48,128]{2,1,0:T(8,128)S(1)}) custom-call(f32[8,136,128]{2,1,0:T(8,128)S(1)} %all_to_all.20.full, f32[32,128]{1,0:T(8,128)S(1)} %get-tuple-element.16.wg, f32[8,128]{1,0:T(8,128)S(1)} %get-tuple-element.17.small), custom_call_target="tpu_custom_call" | custom-call | tf_op jit(solution)/shard_map/own/pallas_call | solution.py:476
  49.1 0.0 copy-start.2
  49.1 12.5 %all_to_all.21.got = f32[8,48,128]{2,1,0:T(8,128)S(1)} all-to-all(f32[8,48,128]{2,1,0:T(8,128)S(1)} %get-tuple-element.18.message), channel_id=1, replica_groups={{0,1,2,3,4,5,6,7},{8,9,10,11,12,13,14,15},{16,17,18,19,20,21,22,23},{24..., dimensions={0} | all-to-all | bytes 393216 | tf_op jit(solution)/shard_map/all_to_all | solution.py:484
  61.6 0.0 copy-done.2
  61.6 1.1 select.1
  62.7 22.7 %all_to_all.22.got = f32[8,144,128]{2,1,0:T(8,128)S(1)} all-to-all(f32[8,144,128]{2,1,0:T(8,128)S(1)} %select.1), channel_id=1, replica_groups={{0,8,16,24,32,40,48,56},{1,9,17,25,33,41,49,57},{2,10,18,26,34,42,50,58..., dimensions={0} | all-to-all | bytes 1179648 | tf_op jit(solution)/shard_map/all_to_all | solution.py:494
  85.4 0.6 collect.1
  86.1 0.0 copy-start
  86.1 8.7 %all_to_all.23.mine = f32[4,184,128]{2,1,0:T(8,128)S(1)} all-to-all(f32[4,184,128]{2,1,0:T(8,128)S(1)} %collect.1), channel_id=1, replica_groups={{0,128,256,384},{64,192,320,448},{1,129,257,385},{65,193,321,449},{2,13..., dimensions={0} | all-to-all | bytes 753664 | tf_op jit(solution)/shard_map/all_to_all | solution.py:504
  94.7 6.7 %collective-permute-start.2 = (f32[4,184,128]{2,1,0:T(8,128)S(1)}, f32[4,184,128]{2,1,0:T(8,128)S(1)}, u32[]{:S(2)}, u32[]{:S(2)}) collective-permute-start(f32[4,184,128]{2,1,0:T(8,128)S(1)} %all_to_all.23.mine), channel_id=1, source_target_pairs={{0,64},{64,0},{128,192},{192,128},{256,320},{320,256},{384,448},{4... | collective-permute-start | bytes 1130504 | tf_op jit(solution)/shard_map/ppermute | solution.py:505
  101.4 1.1 collective-permute-done.2.other
  102.5 0.0 copy-done
  102.5 14.6 %solve.1 = (f32[2048,128]{1,0:T(8,128)}, f32[128,128]{1,0:T(8,128)}) custom-call(s32[64]{0:T(128)S(1)} %copy-done.2, s32[1,2,16]{2,1,0:T(2,128)S(1)} %copy-done.1, f32[4,184,128]{2,1,0:T(8,128)S(1)} %all_to_all.23.mine, f32[4,184,128]{2,1,0:T(8,128)S(1)} %collective-permute-done.2.other, f32[128,128]{1,0:T(8,128)S(1)} %get-tuple-element.19.k_own, ...), custom_call_target="tpu_custom_call" | custom-call | tf_op jit(solution)/shard_map/solve/pallas_call | solution.py:506
Async XLA Ops:
  2.7 19.7 %copy-start.3 = (f32[1,2,16]{2,1,0:T(2,128)S(1)}, f32[1,2,16]{2,1,0:T(2,128)}, u32[]{:S(2)}) copy-start(f32[1,2,16]{2,1,0:T(2,128)} %stiff.1) | copy-start | bytes 388
  2.7 19.7 %copy-start.1 = (s32[1,2,16]{2,1,0:T(2,128)S(1)}, s32[1,2,16]{2,1,0:T(2,128)}, u32[]{:S(2)}) copy-start(s32[1,2,16]{2,1,0:T(2,128)} %index.3) | copy-start | bytes 388
  2.7 14.3 %collective-permute-start.1 = (f32[1552,128]{1,0:T(8,128)S(1)}, f32[1552,128]{1,0:T(8,128)S(1)}, u32[]{:S(2)}, u32[]{:S(2)}) collective-permute-start(f32[1552,128]{1,0:T(8,128)S(1)} %get-tuple-element.13.left), channel_id=1, source_target_pairs={{64,0},{128,64},{192,128},{256,192},{320,256},{384,320},{448,384},... | collective-permute-start | bytes 2383880 | tf_op jit(solution)/shard_map/ppermute | solution.py:462
  11.5 10.9 %collective-permute-start = (f32[1552,128]{1,0:T(8,128)S(1)}, f32[1552,128]{1,0:T(8,128)S(1)}, u32[]{:S(2)}, u32[]{:S(2)}) collective-permute-start(f32[1552,128]{1,0:T(8,128)S(1)} %get-tuple-element.14.right), channel_id=1, source_target_pairs={{0,64},{64,128},{128,192},{192,256},{256,320},{320,384},{384,448},... | collective-permute-start | bytes 2383880 | tf_op jit(solution)/shard_map/ppermute | solution.py:461
  49.1 12.5 %copy-start.2 = (s32[64]{0:T(128)S(1)}, s32[64]{0:T(128)}, u32[]{:S(2)}) copy-start(s32[64]{0:T(128)} %order.5) | copy-start | bytes 772
  86.1 16.5 %copy-start = (f32[384,128]{1,0:T(8,128)S(1)}, f32[384,128]{1,0:T(8,128)}, u32[]{:S(2)}) copy-start(f32[384,128]{1,0:T(8,128)} %start.1) | copy-start | bytes 589828
  94.7 7.8 %collective-permute-start.2 = (f32[4,184,128]{2,1,0:T(8,128)S(1)}, f32[4,184,128]{2,1,0:T(8,128)S(1)}, u32[]{:S(2)}, u32[]{:S(2)}) collective-permute-start(f32[4,184,128]{2,1,0:T(8,128)S(1)} %all_to_all.23.mine), channel_id=1, source_target_pairs={{0,64},{64,0},{128,192},{192,128},{256,320},{320,256},{384,448},{4... | collective-permute-start | bytes 1130504 | tf_op jit(solution)/shard_map/ppermute | solution.py:505

commit v6 on v5

--- a/solution.py
+++ b/solution.py
@@ -141,8 +141,9 @@
     ]
 
 
-def prep_kernel(planes, v_far, rho_far, left, right, v, wide, rho, sems):
+def prep_kernel(planes, v_far, rho_far, chip, link, v, wide, rho, sems):
     h = lax.axis_index("halo")
+    odd = h % 2 == 1
     step = NC // 4
     copies = [
         pltpu.make_async_copy(v_far.at[i * step : (i + 1) * step], v.at[i * step : (i + 1) * step], sems.at[i])
@@ -154,18 +155,18 @@
     for i in range(4):
         copies[i].wait()
         wide[i * step : (i + 1) * step, :] = v[i * step : (i + 1) * step, :].astype(F32)
+        parts = []
         for k in range(16):
             part = wide[pl.ds(i * step + k, NV // 4, stride=16), :]
-            part = jnp.where(h * 4 + k // 4 < planes[0], part, 0.0)
-            at = k * NV + i * (NV // 4)
-            if k < 12:
-                left[at : at + NV // 4, :] = part
-            if k >= 4:
-                right[at - 4 * NV : at - 4 * NV + NV // 4, :] = part
+            parts.append(jnp.where(h * 4 + k // 4 < planes[0], part, 0.0))
+        for k in range(12):
+            at = slice(k * NV + i * (NV // 4), k * NV + (i + 1) * (NV // 4))
+            chip[at, :] = jnp.where(odd, parts[k], parts[k + 4])
+            link[at, :] = jnp.where(odd, parts[k + 4], parts[k])
     copies[4].wait()
-    left[12 * NV :, :] = rho[...]
-    right[12 * NV : 12 * NV + 12, :] = rho[4:, :]
-    right[12 * NV + 12 :, :] = rho[:4, :]
+    lo, hi = rho[...], jnp.concatenate([rho[4:, :], rho[:4, :]], axis=0)
+    chip[12 * NV :, :] = jnp.where(odd, lo, hi)
+    link[12 * NV :, :] = jnp.where(odd, hi, lo)
 
 
 def smooth_first(cells):
@@ -179,7 +180,7 @@
 
 
 def front_kernel(
-    planes, index, stiff, index_v, left, right, from_left, from_right, w_out, full_out, wg_out, tile_out, rho_s, both
+    planes, index, stiff, index_v, chip, link, from_chip, from_link, w_out, full_out, wg_out, tile_out, rho_s, both
 ):
     h = lax.axis_index("halo")
     tile_out[...] = jnp.zeros((8, NV), F32)
@@ -190,20 +191,22 @@
     half_hi = jnp.where(lane == NV - 1, 0.0, 0.5).astype(F32)
     on = [jnp.where((h * 4 + q >= 0) & (h * 4 + q < planes[0]), 1.0 / 64, 0.0) for q in range(-3, 7)]
 
+    odd = h % 2 == 1
+
     def place(q):
         if q < 0:
-            return from_left, q + 3
+            return (from_link, q + 3), (from_chip, q + 3)
         if q < 3:
-            return left, q
+            return (link, q), (chip, q)
         if q == 3:
-            return right, 2
-        return from_right, q - 4
+            return (chip, 2), (link, 2)
+        return (from_chip, q - 4), (from_link, q - 4)
 
     for q in range(-3, 7):
-        ref, p = place(q)
+        (even_ref, p), (odd_ref, _) = place(q)
         for c in range(4):
-            row = 12 * NV + 4 * p + c
-            rho_s[q + 3, c] = jnp.broadcast_to(ref[row : row + 1, :], (8, NV))
+            at = slice(12 * NV + 4 * p + c, 12 * NV + 4 * p + c + 1)
+            rho_s[q + 3, c] = jnp.broadcast_to(jnp.where(odd, odd_ref[at, :], even_ref[at, :]), (8, NV))
 
     def smooth_third(x):
         return x + half_lo * pltpu.roll(x, 1, 1) + half_hi * pltpu.roll(x, NV - 1, 1)
@@ -223,8 +226,9 @@
     def group(g, carry):
         cells = []
         for q in range(-3, 7):
-            ref, p = place(q)
-            cells.append([ref[pl.ds(pl.multiple_of((4 * p + c) * NV + g * 8, 8), 8), :] for c in range(4)])
+            (even_ref, p), (odd_ref, _) = place(q)
+            at = [pl.ds(pl.multiple_of((4 * p + c) * NV + g * 8, 8), 8) for c in range(4)]
+            cells.append([jnp.where(odd, odd_ref[a, :], even_ref[a, :]) for a in at])
         cells = apply(apply(cells, 0), 1)
         rows = pl.ds(pl.multiple_of(32 + g * 8, 8), 8)
         for p in range(4):
@@ -444,7 +448,7 @@
     everyone = ("halo", "leaf")
     chips = [[0, 2, 4, 6], [1, 3, 5, 7]]
     edge = 12 * NV + 16
-    left, right = pl.pallas_call(
+    chip, link = pl.pallas_call(
         prep_kernel,
         out_shape=(shape(edge, NV), shape(edge, NV)),
         in_specs=[SM, FAR, FAR],
@@ -458,8 +462,8 @@
         name="prep",
         compiler_params=grant(8),
     )(planes, far(start_modes.reshape(NC, NV)), far(density.reshape(16, NV)))
-    from_left = lax.ppermute(right, "halo", [(i, i + 1) for i in range(7)])
-    from_right = lax.ppermute(left, "halo", [(i + 1, i) for i in range(7)])
+    from_link = lax.ppermute(link, "halo", [(i, i + 1 if i % 2 else i - 1) for i in range(1, 7)])
+    from_chip = lax.ppermute(chip, "halo", [(i, i ^ 1) for i in range(8)])
     w, full, wg, small = pl.pallas_call(
         front_kernel,
         out_shape=(shape(NV, NC), shape(8, NV + 8, NV), shape(32, NV), shape(8, NV)),
@@ -471,7 +475,7 @@
         ],
         name="front",
         compiler_params=grant(24),
-    )(planes, iface_index, iface_stiff, iface_index, left, right, from_left, from_right)
+    )(planes, iface_index, iface_stiff, iface_index, chip, link, from_chip, from_link)
     full = lax.all_to_all(full, "halo", 0, 0, tiled=True)
     li, k_own, message = pl.pallas_call(
         own_kernel,

time: 117 us -> 118 us (level)
  waiting for transfers between devices: 10.1 us -> 12.6 us
  blocking collectives: 58 us -> 55.6 us
    ppermute x2, waiting for transfers between devices: 9 us -> 11.5 us  [the longest x1 11.5 us: per_device(): lax.ppermute(link, 'halo', [(i, i + 1 if i % 2 else i - 1) for i in range...]
    all_to_all x1, blocking collectives: 14.1 us -> 11.7 us  [per_device(): full = lax.all_to_all(full, 'halo', 0, 0, tiled=True)]
  transfers between devices with their start and end apart: 3 -> 3, of which waited for: 3 -> 2; matrix products, arithmetic and copies ran while one was open for 0% -> 0% of each run, Pallas kernels for 0% -> 0%
where the time goes in v6:
time: 118 us; the launch traced here: 117 us
  blocking collectives  55.6 us (47%)
  Pallas kernels  30.3 us (26%)
  starting transfers between devices  17.3 us (15%)
  waiting for transfers between devices  12.6 us (11%)
  between operations  1.38 us (1%)
    all_to_all x1, blocking collectives, per_device(): lax.all_to_all(chosen, everyone, 0, 0, tiled=True, axis_index_groups=seco...  22.7 us
    pallas_call x1, Pallas kernels, per_device(): pl.pallas_call(solve_kernel, out_shape=(shape(NC, NV), shape(NV, NV)), in...  14.6 us
    all_to_all x1, blocking collectives, per_device(): lax.all_to_all(message, everyone, 0, 0, tiled=True, axis_index_groups=fir...  12.5 us
    all_to_all x1, blocking collectives, per_device(): full = lax.all_to_all(full, 'halo', 0, 0, tiled=True)  11.7 us
    ppermute x1, waiting for transfers between devices, per_device(): lax.ppermute(link, 'halo', [(i, i + 1 if i % 2 else i - 1) for i in range...  11.5 us
    pallas_call x1, Pallas kernels, per_device(): pl.pallas_call(front_kernel, out_shape=(shape(NV, NC), shape(8, NV + 8, N...  8.96 us
    ppermute x1, starting transfers between devices, per_device(): from_chip = lax.ppermute(chip, 'halo', [(i, i ^ 1) for i in range(8)])  8.75 us
    all_to_all x1, blocking collectives, per_device(): lax.all_to_all(gathered, 'halo', 0, 0, tiled=True, axis_index_groups=chips)  8.66 us
  transfers between devices with their start and end apart: 3, of which 2 were waited for; matrix products, arithmetic and copies ran while one was open for 0% of the time, Pallas kernels for 0%

profile of v6, /device:TPU:1, one launch (start us, length us, event | category | flops | bytes accessed | tf_op | source)
XLA Modules:
  0.0 117.2 jit_solution(16428661110420660111)
XLA Ops:
  1.3 1.4 %prep.1 = (f32[1552,128]{1,0:T(8,128)S(1)}, f32[1552,128]{1,0:T(8,128)S(1)}) custom-call(s32[1]{0:T(128)S(6)} %copy.9.planes, bf16[2048,128]{1,0:T(8,128)(2,1)} %bitcast.4, f32[16,128]{1,0:T(8,128)} %bitcast.5), custom_call_target="tpu_custom_call" | custom-call | tf_op jit(solution)/shard_map/prep/pallas_call | solution.py:451
  2.7 0.0 copy-start.3
  2.7 0.0 copy-start.1
  2.7 8.7 %collective-permute-start = (f32[1552,128]{1,0:T(8,128)S(1)}, f32[1552,128]{1,0:T(8,128)S(1)}, u32[]{:S(2)}, u32[]{:S(2)}) collective-permute-start(f32[1552,128]{1,0:T(8,128)S(1)} %get-tuple-element.13.chip), channel_id=1, source_target_pairs={{0,64},{64,0},{128,192},{192,128},{256,320},{320,256},{384,448},{4... | collective-permute-start | bytes 2383880 | tf_op jit(solution)/shard_map/ppermute | solution.py:466
  11.5 1.9 %collective-permute-start.1 = (f32[1552,128]{1,0:T(8,128)S(1)}, f32[1552,128]{1,0:T(8,128)S(1)}, u32[]{:S(2)}, u32[]{:S(2)}) collective-permute-start(f32[1552,128]{1,0:T(8,128)S(1)} %get-tuple-element.14.link), channel_id=1, source_target_pairs={{64,128},{128,64},{192,256},{256,192},{320,384},{384,320},{65,129}... | collective-permute-start | bytes 2383880 | tf_op jit(solution)/shard_map/ppermute | solution.py:465
  13.4 0.0 collective-permute-done.from_chip
  13.4 11.5 %collective-permute-done.1.from_link = f32[1552,128]{1,0:T(8,128)S(1)} collective-permute-done((f32[1552,128]{1,0:T(8,128)S(1)}, f32[1552,128]{1,0:T(8,128)S(1)}, u32[]{:S(2)}, u32[]{:S(2)}) %collective-permute-start.1) | collective-permute-done | bytes 794656 | tf_op jit(solution)/shard_map/ppermute | solution.py:465
  24.9 0.0 copy-done.3
  24.9 0.0 copy-done.1
  24.9 9.0 %front.1 = (f32[128,2048]{1,0:T(8,128)S(1)}, f32[8,136,128]{2,1,0:T(8,128)S(1)}, f32[32,128]{1,0:T(8,128)S(1)}, f32[8,128]{1,0:T(8,128)S(1)}) custom-call(s32[1]{0:T(128)S(6)} %copy.9.planes, s32[1,2,16]{2,1,0:T(2,128)S(1)} %copy-done.1, f32[1,2,16]{2,1,0:T(2,128)S(1)} %copy-done.3, s32[1,2,16]{2,1,0:T(2,128)S(1)} %copy-done.1, ...), custom_call_target="tpu_custom_call" | custom-call | tf_op jit(solution)/shard_map/front/pallas_call | solution.py:467
  33.8 11.7 %all_to_all.20.full = f32[8,136,128]{2,1,0:T(8,128)S(1)} all-to-all(f32[8,136,128]{2,1,0:T(8,128)S(1)} %get-tuple-element.15), channel_id=1, replica_groups=mesh['halo'=8,'leaf'=64] {'halo'}, dimensions={0} | all-to-all | bytes 1114112 | tf_op jit(solution)/shard_map/all_to_all | solution.py:479
  45.5 3.7 %own.1 = (f32[128,128]{1,0:T(8,128)S(1)}, f32[128,128]{1,0:T(8,128)S(1)}, f32[8,48,128]{2,1,0:T(8,128)S(1)}) custom-call(f32[8,136,128]{2,1,0:T(8,128)S(1)} %all_to_all.20.full, f32[32,128]{1,0:T(8,128)S(1)} %get-tuple-element.16.wg, f32[8,128]{1,0:T(8,128)S(1)} %get-tuple-element.17.small), custom_call_target="tpu_custom_call" | custom-call | tf_op jit(solution)/shard_map/own/pallas_call | solution.py:480
  49.2 0.0 copy-start.2
  49.2 12.5 %all_to_all.21.got = f32[8,48,128]{2,1,0:T(8,128)S(1)} all-to-all(f32[8,48,128]{2,1,0:T(8,128)S(1)} %get-tuple-element.18.message), channel_id=1, replica_groups={{0,1,2,3,4,5,6,7},{8,9,10,11,12,13,14,15},{16,17,18,19,20,21,22,23},{24..., dimensions={0} | all-to-all | bytes 393216 | tf_op jit(solution)/shard_map/all_to_all | solution.py:488
  61.8 0.0 copy-done.2
  61.8 1.1 select.1
  62.9 22.7 %all_to_all.22.got = f32[8,144,128]{2,1,0:T(8,128)S(1)} all-to-all(f32[8,144,128]{2,1,0:T(8,128)S(1)} %select.1), channel_id=1, replica_groups={{0,8,16,24,32,40,48,56},{1,9,17,25,33,41,49,57},{2,10,18,26,34,42,50,58..., dimensions={0} | all-to-all | bytes 1179648 | tf_op jit(solution)/shard_map/all_to_all | solution.py:498
  85.5 0.6 collect.1
  86.2 0.0 copy-start
  86.2 8.7 %all_to_all.23.mine = f32[4,184,128]{2,1,0:T(8,128)S(1)} all-to-all(f32[4,184,128]{2,1,0:T(8,128)S(1)} %collect.1), channel_id=1, replica_groups={{0,128,256,384},{64,192,320,448},{1,129,257,385},{65,193,321,449},{2,13..., dimensions={0} | all-to-all | bytes 753664 | tf_op jit(solution)/shard_map/all_to_all | solution.py:508
  94.9 6.7 %collective-permute-start.2 = (f32[4,184,128]{2,1,0:T(8,128)S(1)}, f32[4,184,128]{2,1,0:T(8,128)S(1)}, u32[]{:S(2)}, u32[]{:S(2)}) collective-permute-start(f32[4,184,128]{2,1,0:T(8,128)S(1)} %all_to_all.23.mine), channel_id=1, source_target_pairs={{0,64},{64,0},{128,192},{192,128},{256,320},{320,256},{384,448},{4... | collective-permute-start | bytes 1130504 | tf_op jit(solution)/shard_map/ppermute | solution.py:509
  101.5 1.1 collective-permute-done.2.other
  102.7 0.0 copy-done
  102.7 14.6 %solve.1 = (f32[2048,128]{1,0:T(8,128)}, f32[128,128]{1,0:T(8,128)}) custom-call(s32[64]{0:T(128)S(1)} %copy-done.2, s32[1,2,16]{2,1,0:T(2,128)S(1)} %copy-done.1, f32[4,184,128]{2,1,0:T(8,128)S(1)} %all_to_all.23.mine, f32[4,184,128]{2,1,0:T(8,128)S(1)} %collective-permute-done.2.other, f32[128,128]{1,0:T(8,128)S(1)} %get-tuple-element.19.k_own, ...), custom_call_target="tpu_custom_call" | custom-call | tf_op jit(solution)/shard_map/solve/pallas_call | solution.py:510
Async XLA Ops:
  2.7 22.2 %copy-start.3 = (f32[1,2,16]{2,1,0:T(2,128)S(1)}, f32[1,2,16]{2,1,0:T(2,128)}, u32[]{:S(2)}) copy-start(f32[1,2,16]{2,1,0:T(2,128)} %stiff.1) | copy-start | bytes 388
  2.7 22.2 %copy-start.1 = (s32[1,2,16]{2,1,0:T(2,128)S(1)}, s32[1,2,16]{2,1,0:T(2,128)}, u32[]{:S(2)}) copy-start(s32[1,2,16]{2,1,0:T(2,128)} %index.3) | copy-start | bytes 388
  2.7 10.7 %collective-permute-start = (f32[1552,128]{1,0:T(8,128)S(1)}, f32[1552,128]{1,0:T(8,128)S(1)}, u32[]{:S(2)}, u32[]{:S(2)}) collective-permute-start(f32[1552,128]{1,0:T(8,128)S(1)} %get-tuple-element.13.chip), channel_id=1, source_target_pairs={{0,64},{64,0},{128,192},{192,128},{256,320},{320,256},{384,448},{4... | collective-permute-start | bytes 2383880 | tf_op jit(solution)/shard_map/ppermute | solution.py:466
  11.5 13.4 %collective-permute-start.1 = (f32[1552,128]{1,0:T(8,128)S(1)}, f32[1552,128]{1,0:T(8,128)S(1)}, u32[]{:S(2)}, u32[]{:S(2)}) collective-permute-start(f32[1552,128]{1,0:T(8,128)S(1)} %get-tuple-element.14.link), channel_id=1, source_target_pairs={{64,128},{128,64},{192,256},{256,192},{320,384},{384,320},{65,129}... | collective-permute-start | bytes 2383880 | tf_op jit(solution)/shard_map/ppermute | solution.py:465
  49.2 12.5 %copy-start.2 = (s32[64]{0:T(128)S(1)}, s32[64]{0:T(128)}, u32[]{:S(2)}) copy-start(s32[64]{0:T(128)} %order.5) | copy-start | bytes 772
  86.2 16.5 %copy-start = (f32[384,128]{1,0:T(8,128)S(1)}, f32[384,128]{1,0:T(8,128)}, u32[]{:S(2)}) copy-start(f32[384,128]{1,0:T(8,128)} %start.1) | copy-start | bytes 589828
  94.9 7.8 %collective-permute-start.2 = (f32[4,184,128]{2,1,0:T(8,128)S(1)}, f32[4,184,128]{2,1,0:T(8,128)S(1)}, u32[]{:S(2)}, u32[]{:S(2)}) collective-permute-start(f32[4,184,128]{2,1,0:T(8,128)S(1)} %all_to_all.23.mine), channel_id=1, source_target_pairs={{0,64},{64,0},{128,192},{192,128},{256,320},{320,256},{384,448},{4... | collective-permute-start | bytes 1130504 | tf_op jit(solution)/shard_map/ppermute | solution.py:509
